TPU v7x, 128 devices: a whole 4x4x4 slice. The times are simulated.
128 devices in a mesh: row: 8 (over z_hi, y), col: 16 (over z_lo, x, core).
Axes of the slice: x: 4, y: 4, z: 4 (z_hi: 2, z_lo: 2; z = z_hi * 2 + z_lo), core: 2. Of those that a mesh axis runs over, the one named last changes fastest.
Arguments:
- gram: float32 [8192, 8192], P('row', 'col'), may hold values from -6 to 8
- rotations: float32 [2, 8, 1024, 1024], P(None, 'row', 'col'), may hold values from -1 to 2
Outputs:
- rotated: float32 [8192, 8192], P('row', 'col')
All inputs are finite; a program needn't handle non-finite values.
Results may differ from a plain program's by a relative error of at most 0.00016.
Values sent between devices are 32-bit elements; how exact they have to be, the bound alone decides.
No kernel may reach another device: no remote copies, remote signals or barrier semaphores. Data moves between devices by JAX's collectives and lax.ppermute only.
A program may use at most 64 MiB of HBM per device.

v0:
```python
import jax
import jax.numpy as jnp
from jax import lax
from jax.experimental import pallas as pl
from jax.experimental.pallas import tpu as pltpu
from jax.sharding import PartitionSpec as P


N = 512
H = 256
F32 = jnp.float32
HIGH = lax.Precision.HIGH


def place(index):
    row, col = divmod(index, 16)
    return (row // 4, row % 4, col // 8, (col // 2) % 4, col % 2)


def index_of(z_hi, y, z_lo, x, core):
    return (z_hi * 4 + y % 4) * 16 + z_lo * 8 + (x % 4) * 2 + core


def pairs_of(move):
    return [(i, index_of(*move(*place(i)))) for i in range(128)]


def along_x(step):
    return pairs_of(lambda zh, y, zl, x, c: (zh, y, zl, x + step, c))


def along_y(step):
    return pairs_of(lambda zh, y, zl, x, c: (zh, y + step, zl, x, c))


OTHER_LO = pairs_of(lambda zh, y, zl, x, c: (zh, y, 1 - zl, x, c))
OTHER_HI = pairs_of(lambda zh, y, zl, x, c: (1 - zh, y, zl, x, c))
OTHER_CORE = pairs_of(lambda zh, y, zl, x, c: (zh, y, zl, x, 1 - c))
TRANSPOSE = pairs_of(lambda zh, y, zl, x, c: (zl, x, zh, y, c))


def new_position(old):
    if old == 0:
        return 0
    if old == 1:
        return 2
    if old == 14:
        return 15
    return old + 2 if old % 2 == 0 else old - 2


MOVE_COL = [(r * 16 + c, r * 16 + new_position(c)) for r in range(8) for c in range(16)]
ROW_UP = [(r * 16 + c, (r + 1) * 16 + c) for r in range(7) for c in range(16)]
ROW_DOWN = [(r * 16 + c, (r - 1) * 16 + c) for r in range(1, 8) for c in range(16)]


def send(value, pairs):
    return lax.ppermute(value, ("row", "col"), pairs)


def vmem_call(body, inputs, outs):
    return pl.pallas_call(
        body,
        out_shape=[jax.ShapeDtypeStruct(shape, F32) for shape in outs],
        in_specs=[pl.BlockSpec(memory_space=pltpu.VMEM)] * len(inputs),
        out_specs=[pl.BlockSpec(memory_space=pltpu.VMEM)] * len(outs),
        compiler_params=pltpu.CompilerParams(vmem_limit_bytes=12 * 2**20),
        cost_estimate=pl.CostEstimate(flops=0, bytes_accessed=2**22, transcendentals=0),
    )(*inputs)


def rows_body(*refs):
    pieces, out = refs[:4], refs[4]
    col = lax.axis_index("col")
    ring, plane = (col // 2) % 4, col // 8
    for j, piece in enumerate(pieces):
        for part in range(4):
            at = (plane if part < 2 else 1 - plane) * 4 + (ring + j) % 4
            first = at * 128 + 64 * jnp.where(col % 2 == 0, part % 2, 1 - part % 2)
            rows = pl.ds(pl.multiple_of(first, 64), 64)
            out[rows, :] = piece[part * 64 : part * 64 + 64, :]


def join_body(own, other, out):
    up_is_own = (lax.axis_index("col") % 2 == 0) != (lax.axis_index("row") == 0)

    @pl.when(up_is_own)
    def _():
        out[:, 0:N] = own[...]
        out[:, N:] = other[...]

    @pl.when(jnp.logical_not(up_is_own))
    def _():
        out[:, 0:N] = other[...]
        out[:, N:] = own[...]


def cols_body(*refs):
    pieces, own, other = refs[:4], refs[4:6], refs[6:8]
    row, core = lax.axis_index("row"), lax.axis_index("col") % 2
    ring, plane = row % 4, row // 4

    def fill(first, second):
        for j, piece in enumerate(pieces):
            for part in range(4):
                at = (ring + j) % 4 * 128 + 64 * jnp.where(core == 0, part % 2, 1 - part % 2)
                rows = pl.ds(pl.multiple_of(at, 64), 64)
                taken = slice(part * 64, part * 64 + 64)
                for half, out in enumerate(first if part < 2 else second):
                    out[rows, :] = piece[taken, half * H : half * H + H]

    @pl.when(plane == core)
    def _():
        fill(own, other)

    @pl.when(plane != core)
    def _():
        fill(other, own)


def mix(turn, tile):
    dims = (((0,), (0,)), ((), ()))
    return lax.dot_general(turn, tile, dims, precision=HIGH, preferred_element_type=F32)


def times(tile, turn):
    return jnp.dot(tile, turn, precision=HIGH, preferred_element_type=F32)


ROW_RING = (along_x(1), along_x(-1), along_x(2), OTHER_LO)
COL_RING = (along_y(1), along_y(-1), along_y(2), OTHER_HI)


def gather(own, ring):
    forward, backward, opposite, other = ring
    to = lambda value, pairs: send(value, pairs)
    both = jnp.concatenate([own, to(own, other)])
    before = to(both, forward)
    behind = to(both, backward)
    return [both, behind, to(both, opposite), before]


def shards(gram, rotations):
    row = lax.axis_index("row")
    core = lax.axis_index("col") % 2
    keep = lax.dynamic_slice_in_dim(rotations[:, 0], core * N, N, 2)
    give = lax.dynamic_slice_in_dim(rotations[:, 0], (1 - core) * N, N, 2)
    got = send(give, OTHER_CORE)

    def turns(step):
        at = int(step) - 1
        piece = jnp.concatenate([keep[at], got[at]])
        turned = send(piece, TRANSPOSE)
        (half,) = vmem_call(rows_body, gather(piece, ROW_RING), [(2 * N, N)])
        other = send(half, OTHER_CORE)
        (whole,) = vmem_call(join_body, (half, other), [(2 * N, 2 * N)])
        pieces = gather(turned, COL_RING)
        return whole, vmem_call(cols_body, pieces, [(N, H)] * 4)

    def advance(tile, rows, cols):
        own_a, own_b, other_a, other_b = cols
        mixed = mix(rows, tile)
        other = send(mixed, OTHER_CORE)
        own_parts = times(mixed, own_a), times(mixed[:N], own_b), times(mixed[N:], own_b)
        both, up, down = lax.optimization_barrier(own_parts)
        both = both + times(other, other_a)
        up = up + times(other[:N], other_b)
        down = down + times(other[N:], other_b)
        moved = send(both, MOVE_COL)
        row_up = send(up, ROW_UP)
        row_down = send(down, ROW_DOWN)
        moved_up = send(moved[:N], ROW_UP)
        moved_down = send(moved[N:], ROW_DOWN)
        row_up = jnp.where(row == 0, down, row_up)
        row_down = jnp.where(row == 7, up, row_down)
        right = send(jnp.concatenate([row_up, row_down]), MOVE_COL)
        first = jnp.where(row == 0, moved[N:], moved_up)
        second = jnp.where(row == 7, moved[:N], moved_down)
        return jnp.concatenate([jnp.concatenate([first, second]), right], axis=1)

    tile = gram
    for step in ("1", "2"):
        tile = advance(tile, *turns(step))
    return tile


def solution(mesh):
    placed = (P("row", "col"), P(None, "row", "col", None))
    return jax.shard_map(
        shards, mesh=mesh, in_specs=placed, out_specs=P("row", "col"), check_vma=False
    )
```

profile of v0, /device:TPU:24, one launch (start us, length us, event | category | flops | bytes accessed | tf_op | source)
XLA Modules:
  0.0 296.3 jit_solution(3065443340759642183)
XLA Ops:
  2.8 2.0 collective-permute-start.6
  4.8 6.6 %collective-permute-done.6 = f32[128,512]{1,0:T(8,128)S(1)} collective-permute-done((f32[128,512]{1,0:T(8,128)S(1)}, f32[128,512]{1,0:T(8,128)S(1)}, u32[]{:S(2)}, u32[]{:S(2)}) %collective-permute-start.6) | collective-permute-done | bytes 262176 | tf_op jit(solution)/shard_map/ppermute | solution.py:58
  11.4 2.8 collective-permute-start.7
  15.9 20.4 %collective-permute-done.7.refs_1_ = f32[256,512]{1,0:T(8,128)S(1)} collective-permute-done((f32[256,512]{1,0:T(8,128)S(1)}, f32[256,512]{1,0:T(8,128)S(1)}, u32[]{:S(2)}, u32[]{:S(2)}) %collective-permute-start.7) | collective-permute-done | bytes 524320 | tf_op jit(solution)/shard_map/ppermute | solution.py:58
  36.3 3.7 %collective-permute-done.9.refs_3_ = f32[256,512]{1,0:T(8,128)S(1)} collective-permute-done((f32[256,512]{1,0:T(8,128)S(1)}, f32[256,512]{1,0:T(8,128)S(1)}, u32[]{:S(2)}, u32[]{:S(2)}) %collective-permute-start.9) | collective-permute-done | bytes 524320 | tf_op jit(solution)/shard_map/ppermute | solution.py:58
  41.9 2.5 collective-permute-done.10.other
  44.7 3.6 %fusion.21 = f32[1024,512]{1,0:T(8,128)S(1)} fusion(f32[1024,1024]{1,0:T(8,128)S(1)} %shard_map.31, f32[1024,512]{1,0:T(8,128)S(1)} %copy-done), kind=kOutput, calls=%fused_computation.51 | convolution fusion | flops 3221225472 | bytes 8388608 | tf_op jit(solution)/shard_map/dot_general | solution.py:123
  48.5 2.2 collective-permute-start.11
  50.8 3.9 %collective-permute-start.3 = (f32[256,512]{1,0:T(8,128)S(1)}, f32[256,512]{1,0:T(8,128)S(1)}, u32[]{:S(2)}, u32[]{:S(2)}) collective-permute-start(f32[256,512]{1,0:T(8,128)S(1)} %pad_maximum_fusion.3.refs_0_), channel_id=1, source_target_pairs={{0,4},{1,5},{2,6},{3,7},{4,0},{5,1},{6,2},{7,3},{8,12},{9,13},{10,... | collective-permute-start | bytes 1572872 | tf_op jit(solution)/shard_map/ppermute | solution.py:58
  54.7 24.4 %collective-permute-done.11 = f32[128,512]{1,0:T(8,128)S(1)} collective-permute-done((f32[128,512]{1,0:T(8,128)S(1)}, f32[128,512]{1,0:T(8,128)S(1)}, u32[]{:S(2)}, u32[]{:S(2)}) %collective-permute-start.11) | collective-permute-done | bytes 262176 | tf_op jit(solution)/shard_map/ppermute | solution.py:58
  79.1 4.4 %collective-permute-start.12 = (f32[128,512]{1,0:T(8,128)S(1)}, f32[128,512]{1,0:T(8,128)S(1)}, u32[]{:S(2)}, u32[]{:S(2)}) collective-permute-start(f32[128,512]{1,0:T(8,128)S(1)} %collective-permute-done.11), channel_id=1, source_target_pairs={{0,64},{1,65},{2,66},{3,67},{4,68},{5,69},{6,70},{7,71},{8,72},{9,... | collective-permute-start | bytes 786440 | tf_op jit(solution)/shard_map/ppermute | solution.py:58
  83.6 6.0 %collective-permute-done.12 = f32[128,512]{1,0:T(8,128)S(1)} collective-permute-done((f32[128,512]{1,0:T(8,128)S(1)}, f32[128,512]{1,0:T(8,128)S(1)}, u32[]{:S(2)}, u32[]{:S(2)}) %collective-permute-start.12) | collective-permute-done | bytes 262176 | tf_op jit(solution)/shard_map/ppermute | solution.py:58
  89.8 3.2 %collective-permute-start.15 = (f32[256,512]{1,0:T(8,128)S(1)}, f32[256,512]{1,0:T(8,128)S(1)}, u32[]{:S(2)}, u32[]{:S(2)}) collective-permute-start(f32[256,512]{1,0:T(8,128)S(1)} %constant_dynamic-update-slice_fusion.refs_0_), channel_id=1, source_target_pairs={{0,16},{1,17},{2,18},{3,19},{4,20},{5,21},{6,22},{7,23},{8,24},{9,... | collective-permute-start | bytes 1572872 | tf_op jit(solution)/shard_map/ppermute | solution.py:58
  93.0 4.9 %collective-permute-done.4.refs_3_ = f32[256,512]{1,0:T(8,128)S(1)} collective-permute-done((f32[256,512]{1,0:T(8,128)S(1)}, f32[256,512]{1,0:T(8,128)S(1)}, u32[]{:S(2)}, u32[]{:S(2)}) %collective-permute-start.4) | collective-permute-done | bytes 524320 | tf_op jit(solution)/shard_map/ppermute | solution.py:58
  98.1 16.8 %collective-permute-done.13.refs_1_ = f32[256,512]{1,0:T(8,128)S(1)} collective-permute-done((f32[256,512]{1,0:T(8,128)S(1)}, f32[256,512]{1,0:T(8,128)S(1)}, u32[]{:S(2)}, u32[]{:S(2)}) %collective-permute-start.13) | collective-permute-done | bytes 524320 | tf_op jit(solution)/shard_map/ppermute | solution.py:58
  123.4 6.7 %collective-permute-start.20 = (f32[512,256]{1,0:T(8,128)}, f32[512,256]{1,0:T(8,128)}, u32[]{:S(2)}, u32[]{:S(2)}) collective-permute-start(f32[512,256]{1,0:T(8,128)} %convolution_add_fusion.4), channel_id=1, source_target_pairs={{0,16},{1,17},{2,18},{3,19},{4,20},{5,21},{6,22},{7,23},{8,24},{9,... | collective-permute-start | bytes 1572872 | tf_op jit(solution)/shard_map/ppermute | solution.py:58
  133.4 15.2 %collective-permute-done.20 = f32[512,256]{1,0:T(8,128)} collective-permute-done((f32[512,256]{1,0:T(8,128)}, f32[512,256]{1,0:T(8,128)}, u32[]{:S(2)}, u32[]{:S(2)}) %collective-permute-start.20) | collective-permute-done | bytes 524320 | tf_op jit(solution)/shard_map/ppermute | solution.py:58
  149.7 2.8 collective-permute-done.21
  154.6 5.3 %collective-permute-start.18 = (f32[512,256]{1,0:T(8,128)S(1)}, f32[512,256]{1,0:T(8,128)S(1)}, u32[]{:S(2)}, u32[]{:S(2)}) collective-permute-start(f32[512,256]{1,0:T(8,128)S(1)} %get-tuple-element.39), channel_id=1, source_target_pairs={{0,16},{1,17},{2,18},{3,19},{4,20},{5,21},{6,22},{7,23},{8,24},{9,... | collective-permute-start | bytes 1572872 | tf_op jit(solution)/shard_map/ppermute | solution.py:58
  163.6 8.5 %collective-permute-done.18 = f32[512,256]{1,0:T(8,128)S(1)} collective-permute-done((f32[512,256]{1,0:T(8,128)S(1)}, f32[512,256]{1,0:T(8,128)S(1)}, u32[]{:S(2)}, u32[]{:S(2)}) %collective-permute-start.18) | collective-permute-done | bytes 524320 | tf_op jit(solution)/shard_map/ppermute | solution.py:58
  172.1 6.9 %collective-permute-done.19 = f32[512,256]{1,0:T(8,128)S(1)} collective-permute-done((f32[512,256]{1,0:T(8,128)S(1)}, f32[512,256]{1,0:T(8,128)S(1)}, u32[]{:S(2)}, u32[]{:S(2)}) %collective-permute-start.19) | collective-permute-done | bytes 524320 | tf_op jit(solution)/shard_map/ppermute | solution.py:58
  179.2 3.4 %fusion = f32[1024,512]{1,0:T(8,128)S(1)} fusion(f32[1024,1024]{1,0:T(8,128)S(1)} %shard_map.29, f32[1024,256]{1,0:T(8,128)S(1)} %collective-permute-done.22, f32[512,256]{1,0:T(8,128)S(1)} %get-tuple-element.38, f32[512,256]{1,0:T(8,128)S(1)} %get-tuple-element.37), kind=kOutput, calls=%fused_computation | convolution fusion | flops 3222274048 | bytes 8388608 | tf_op jit(solution)/shard_map/dot_general | solution.py:123
  184.6 14.0 %collective-permute-done.23 = f32[128,512]{1,0:T(8,128)S(1)} collective-permute-done((f32[128,512]{1,0:T(8,128)S(1)}, f32[128,512]{1,0:T(8,128)S(1)}, u32[]{:S(2)}, u32[]{:S(2)}) %collective-permute-start.23) | collective-permute-done | bytes 262176 | tf_op jit(solution)/shard_map/ppermute | solution.py:58
  198.7 9.8 %collective-permute-done.24 = f32[128,512]{1,0:T(8,128)S(1)} collective-permute-done((f32[128,512]{1,0:T(8,128)S(1)}, f32[128,512]{1,0:T(8,128)S(1)}, u32[]{:S(2)}, u32[]{:S(2)}) %collective-permute-start.24) | collective-permute-done | bytes 262176 | tf_op jit(solution)/shard_map/ppermute | solution.py:58
  208.6 3.1 %collective-permute-start.27 = (f32[256,512]{1,0:T(8,128)S(1)}, f32[256,512]{1,0:T(8,128)S(1)}, u32[]{:S(2)}, u32[]{:S(2)}) collective-permute-start(f32[256,512]{1,0:T(8,128)S(1)} %constant_dynamic-update-slice_fusion.2.refs_0_), channel_id=1, source_target_pairs={{0,16},{1,17},{2,18},{3,19},{4,20},{5,21},{6,22},{7,23},{8,24},{9,... | collective-permute-start | bytes 1572872 | tf_op jit(solution)/shard_map/ppermute | solution.py:58
  211.8 22.2 %collective-permute-done.25.refs_1_ = f32[256,512]{1,0:T(8,128)S(1)} collective-permute-done((f32[256,512]{1,0:T(8,128)S(1)}, f32[256,512]{1,0:T(8,128)S(1)}, u32[]{:S(2)}, u32[]{:S(2)}) %collective-permute-start.25) | collective-permute-done | bytes 524320 | tf_op jit(solution)/shard_map/ppermute | solution.py:58
  239.6 4.2 %collective-permute-start.32 = (f32[512,256]{1,0:T(8,128)S(1)}, f32[512,256]{1,0:T(8,128)S(1)}, u32[]{:S(2)}, u32[]{:S(2)}) collective-permute-start(f32[512,256]{1,0:T(8,128)S(1)} %convolution_add_fusion.2), channel_id=1, source_target_pairs={{0,16},{1,17},{2,18},{3,19},{4,20},{5,21},{6,22},{7,23},{8,24},{9,... | collective-permute-start | bytes 1572872 | tf_op jit(solution)/shard_map/ppermute | solution.py:58
  246.4 16.1 %collective-permute-done.32 = f32[512,256]{1,0:T(8,128)S(1)} collective-permute-done((f32[512,256]{1,0:T(8,128)S(1)}, f32[512,256]{1,0:T(8,128)S(1)}, u32[]{:S(2)}, u32[]{:S(2)}) %collective-permute-start.32) | collective-permute-done | bytes 524320 | tf_op jit(solution)/shard_map/ppermute | solution.py:58
  262.6 3.9 %collective-permute-done.33 = f32[512,256]{1,0:T(8,128)S(1)} collective-permute-done((f32[512,256]{1,0:T(8,128)S(1)}, f32[512,256]{1,0:T(8,128)S(1)}, u32[]{:S(2)}, u32[]{:S(2)}) %collective-permute-start.33) | collective-permute-done | bytes 524320 | tf_op jit(solution)/shard_map/ppermute | solution.py:58
  267.4 6.3 %collective-permute-start.30 = (f32[512,256]{1,0:T(8,128)S(1)}, f32[512,256]{1,0:T(8,128)S(1)}, u32[]{:S(2)}, u32[]{:S(2)}) collective-permute-start(f32[512,256]{1,0:T(8,128)S(1)} %get-tuple-element.35), channel_id=1, source_target_pairs={{0,16},{1,17},{2,18},{3,19},{4,20},{5,21},{6,22},{7,23},{8,24},{9,... | collective-permute-start | bytes 1572872 | tf_op jit(solution)/shard_map/ppermute | solution.py:58
  275.7 10.3 %collective-permute-done.30 = f32[512,256]{1,0:T(8,128)S(1)} collective-permute-done((f32[512,256]{1,0:T(8,128)S(1)}, f32[512,256]{1,0:T(8,128)S(1)}, u32[]{:S(2)}, u32[]{:S(2)}) %collective-permute-start.30) | collective-permute-done | bytes 524320 | tf_op jit(solution)/shard_map/ppermute | solution.py:58
  286.0 7.7 %collective-permute-done.31 = f32[512,256]{1,0:T(8,128)S(1)} collective-permute-done((f32[512,256]{1,0:T(8,128)S(1)}, f32[512,256]{1,0:T(8,128)S(1)}, u32[]{:S(2)}, u32[]{:S(2)}) %collective-permute-start.31) | collective-permute-done | bytes 524320 | tf_op jit(solution)/shard_map/ppermute | solution.py:58
  (84 shorter events, 41.8 us)
Async XLA Ops:
  11.4 24.9 %collective-permute-start.7 = (f32[256,512]{1,0:T(8,128)S(1)}, f32[256,512]{1,0:T(8,128)S(1)}, u32[]{:S(2)}, u32[]{:S(2)}) collective-permute-start(f32[256,512]{1,0:T(8,128)S(1)} %pad_maximum_fusion.4.refs_0_), channel_id=1, source_target_pairs={{0,6},{1,7},{2,0},{3,1},{4,2},{5,3},{6,4},{7,5},{8,14},{9,15},{10,... | collective-permute-start | bytes 1572872 | tf_op jit(solution)/shard_map/ppermute | solution.py:58
  14.3 22.1 %collective-permute-start.8 = (f32[256,512]{1,0:T(8,128)S(1)}, f32[256,512]{1,0:T(8,128)S(1)}, u32[]{:S(2)}, u32[]{:S(2)}) collective-permute-start(f32[256,512]{1,0:T(8,128)S(1)} %pad_maximum_fusion.4.refs_0_), channel_id=1, source_target_pairs={{0,4},{1,5},{2,6},{3,7},{4,0},{5,1},{6,2},{7,3},{8,12},{9,13},{10,... | collective-permute-start | bytes 1572872 | tf_op jit(solution)/shard_map/ppermute | solution.py:58
  15.1 24.9 %collective-permute-start.9 = (f32[256,512]{1,0:T(8,128)S(1)}, f32[256,512]{1,0:T(8,128)S(1)}, u32[]{:S(2)}, u32[]{:S(2)}) collective-permute-start(f32[256,512]{1,0:T(8,128)S(1)} %pad_maximum_fusion.4.refs_0_), channel_id=1, source_target_pairs={{0,2},{1,3},{2,4},{3,5},{4,6},{5,7},{6,0},{7,1},{8,10},{9,11},{10,... | collective-permute-start | bytes 1572872 | tf_op jit(solution)/shard_map/ppermute | solution.py:58
  40.3 10.4 %collective-permute-start.1 = (f32[128,512]{1,0:T(8,128)S(1)}, f32[128,512]{1,0:T(8,128)S(1)}, u32[]{:S(2)}, u32[]{:S(2)}) collective-permute-start(f32[128,512]{1,0:T(8,128)S(1)} %pad_maximum_fusion.5), channel_id=1, source_target_pairs={{0,8},{1,9},{2,10},{3,11},{4,12},{5,13},{6,14},{7,15},{8,0},{9,1},... | collective-permute-start | bytes 786440 | tf_op jit(solution)/shard_map/ppermute | solution.py:58
  48.3 69.8 %collective-permute-start.16 = (f32[1024,512]{1,0:T(8,128)S(1)}, f32[1024,512]{1,0:T(8,128)S(1)}, u32[]{:S(2)}, u32[]{:S(2)}) collective-permute-start(f32[1024,512]{1,0:T(8,128)S(1)} %fusion.21), channel_id=1, source_target_pairs={{0,1},{1,0},{2,3},{3,2},{4,5},{5,4},{6,7},{7,6},{8,9},{9,8},{10,11... | collective-permute-start | bytes 6291464 | tf_op jit(solution)/shard_map/ppermute | solution.py:58
  48.5 30.6 %collective-permute-start.11 = (f32[128,512]{1,0:T(8,128)S(1)}, f32[128,512]{1,0:T(8,128)S(1)}, u32[]{:S(2)}, u32[]{:S(2)}) collective-permute-start(f32[128,512]{1,0:T(8,128)S(1)} %pad_maximum_fusion.6), channel_id=1, source_target_pairs={{0,0},{1,1},{2,16},{3,17},{4,32},{5,33},{6,48},{7,49},{8,64},{9,65... | collective-permute-start | bytes 786440 | tf_op jit(solution)/shard_map/ppermute | solution.py:58
  50.7 39.0 %collective-permute-start.2 = (f32[256,512]{1,0:T(8,128)S(1)}, f32[256,512]{1,0:T(8,128)S(1)}, u32[]{:S(2)}, u32[]{:S(2)}) collective-permute-start(f32[256,512]{1,0:T(8,128)S(1)} %pad_maximum_fusion.3.refs_0_), channel_id=1, source_target_pairs={{0,6},{1,7},{2,0},{3,1},{4,2},{5,3},{6,4},{7,5},{8,14},{9,15},{10,... | collective-permute-start | bytes 1572872 | tf_op jit(solution)/shard_map/ppermute | solution.py:58
  50.8 39.0 %collective-permute-start.3 = (f32[256,512]{1,0:T(8,128)S(1)}, f32[256,512]{1,0:T(8,128)S(1)}, u32[]{:S(2)}, u32[]{:S(2)}) collective-permute-start(f32[256,512]{1,0:T(8,128)S(1)} %pad_maximum_fusion.3.refs_0_), channel_id=1, source_target_pairs={{0,4},{1,5},{2,6},{3,7},{4,0},{5,1},{6,2},{7,3},{8,12},{9,13},{10,... | collective-permute-start | bytes 1572872 | tf_op jit(solution)/shard_map/ppermute | solution.py:58
  79.1 10.4 %collective-permute-start.12 = (f32[128,512]{1,0:T(8,128)S(1)}, f32[128,512]{1,0:T(8,128)S(1)}, u32[]{:S(2)}, u32[]{:S(2)}) collective-permute-start(f32[128,512]{1,0:T(8,128)S(1)} %collective-permute-done.11), channel_id=1, source_target_pairs={{0,64},{1,65},{2,66},{3,67},{4,68},{5,69},{6,70},{7,71},{8,72},{9,... | collective-permute-start | bytes 786440 | tf_op jit(solution)/shard_map/ppermute | solution.py:58
  83.5 14.3 %collective-permute-start.4 = (f32[256,512]{1,0:T(8,128)S(1)}, f32[256,512]{1,0:T(8,128)S(1)}, u32[]{:S(2)}, u32[]{:S(2)}) collective-permute-start(f32[256,512]{1,0:T(8,128)S(1)} %pad_maximum_fusion.3.refs_0_), channel_id=1, source_target_pairs={{0,2},{1,3},{2,4},{3,5},{4,6},{5,7},{6,0},{7,1},{8,10},{9,11},{10,... | collective-permute-start | bytes 1572872 | tf_op jit(solution)/shard_map/ppermute | solution.py:58
  89.6 25.3 %collective-permute-start.13 = (f32[256,512]{1,0:T(8,128)S(1)}, f32[256,512]{1,0:T(8,128)S(1)}, u32[]{:S(2)}, u32[]{:S(2)}) collective-permute-start(f32[256,512]{1,0:T(8,128)S(1)} %constant_dynamic-update-slice_fusion.refs_0_), channel_id=1, source_target_pairs={{0,48},{1,49},{2,50},{3,51},{4,52},{5,53},{6,54},{7,55},{8,56},{9,... | collective-permute-start | bytes 1572872 | tf_op jit(solution)/shard_map/ppermute | solution.py:58
  89.7 25.2 %collective-permute-start.14 = (f32[256,512]{1,0:T(8,128)S(1)}, f32[256,512]{1,0:T(8,128)S(1)}, u32[]{:S(2)}, u32[]{:S(2)}) collective-permute-start(f32[256,512]{1,0:T(8,128)S(1)} %constant_dynamic-update-slice_fusion.refs_0_), channel_id=1, source_target_pairs={{0,32},{1,33},{2,34},{3,35},{4,36},{5,37},{6,38},{7,39},{8,40},{9,... | collective-permute-start | bytes 1572872 | tf_op jit(solution)/shard_map/ppermute | solution.py:58
  89.8 25.7 %collective-permute-start.15 = (f32[256,512]{1,0:T(8,128)S(1)}, f32[256,512]{1,0:T(8,128)S(1)}, u32[]{:S(2)}, u32[]{:S(2)}) collective-permute-start(f32[256,512]{1,0:T(8,128)S(1)} %constant_dynamic-update-slice_fusion.refs_0_), channel_id=1, source_target_pairs={{0,16},{1,17},{2,18},{3,19},{4,20},{5,21},{6,22},{7,23},{8,24},{9,... | collective-permute-start | bytes 1572872 | tf_op jit(solution)/shard_map/ppermute | solution.py:58
  98.0 63.7 %collective-permute-start.5 = (f32[1024,512]{1,0:T(8,128)S(1)}, f32[1024,512]{1,0:T(8,128)}, u32[]{:S(2)}, u32[]{:S(2)}) collective-permute-start(f32[1024,512]{1,0:T(8,128)S(1)} %shard_map.28.own), channel_id=1, source_target_pairs={{0,1},{1,0},{2,3},{3,2},{4,5},{5,4},{6,7},{7,6},{8,9},{9,8},{10,11... | collective-permute-start | bytes 6291464 | tf_op jit(solution)/shard_map/ppermute | solution.py:58
  120.1 34.4 %collective-permute-start.17 = (f32[1024,256]{1,0:T(8,128)}, f32[1024,256]{1,0:T(8,128)S(1)}, u32[]{:S(2)}, u32[]{:S(2)}) collective-permute-start(f32[1024,256]{1,0:T(8,128)} %convolution_add_fusion.1), channel_id=1, source_target_pairs={{0,0},{1,2},{2,4},{3,1},{4,6},{5,3},{6,8},{7,5},{8,10},{9,7},{10,1... | collective-permute-start | bytes 3145736 | tf_op jit(solution)/shard_map/ppermute | solution.py:58
  123.4 25.3 %collective-permute-start.20 = (f32[512,256]{1,0:T(8,128)}, f32[512,256]{1,0:T(8,128)}, u32[]{:S(2)}, u32[]{:S(2)}) collective-permute-start(f32[512,256]{1,0:T(8,128)} %convolution_add_fusion.4), channel_id=1, source_target_pairs={{0,16},{1,17},{2,18},{3,19},{4,20},{5,21},{6,22},{7,23},{8,24},{9,... | collective-permute-start | bytes 1572872 | tf_op jit(solution)/shard_map/ppermute | solution.py:58
  131.5 21.1 %collective-permute-start.21 = (f32[512,256]{1,0:T(8,128)}, f32[512,256]{1,0:T(8,128)}, u32[]{:S(2)}, u32[]{:S(2)}) collective-permute-start(f32[512,256]{1,0:T(8,128)} %convolution_add_fusion.5), channel_id=1, source_target_pairs={{16,0},{17,1},{18,2},{19,3},{20,4},{21,5},{22,6},{23,7},{24,8},{25... | collective-permute-start | bytes 1572872 | tf_op jit(solution)/shard_map/ppermute | solution.py:58
  153.7 25.4 %collective-permute-start.22 = (f32[1024,256]{1,0:T(8,128)S(1)}, f32[1024,256]{1,0:T(8,128)S(1)}, u32[]{:S(2)}, u32[]{:S(2)}) collective-permute-start(f32[1024,256]{1,0:T(8,128)S(1)} %pad_maximum_fusion.1), channel_id=1, source_target_pairs={{0,0},{1,2},{2,4},{3,1},{4,6},{5,3},{6,8},{7,5},{8,10},{9,7},{10,1... | collective-permute-start | bytes 3145736 | tf_op jit(solution)/shard_map/ppermute | solution.py:58
  154.6 17.6 %collective-permute-start.18 = (f32[512,256]{1,0:T(8,128)S(1)}, f32[512,256]{1,0:T(8,128)S(1)}, u32[]{:S(2)}, u32[]{:S(2)}) collective-permute-start(f32[512,256]{1,0:T(8,128)S(1)} %get-tuple-element.39), channel_id=1, source_target_pairs={{0,16},{1,17},{2,18},{3,19},{4,20},{5,21},{6,22},{7,23},{8,24},{9,... | collective-permute-start | bytes 1572872 | tf_op jit(solution)/shard_map/ppermute | solution.py:58
  159.8 19.2 %collective-permute-start.19 = (f32[512,256]{1,0:T(8,128)S(1)}, f32[512,256]{1,0:T(8,128)S(1)}, u32[]{:S(2)}, u32[]{:S(2)}) collective-permute-start(f32[512,256]{1,0:T(8,128)S(1)} %get-tuple-element.40), channel_id=1, source_target_pairs={{16,0},{17,1},{18,2},{19,3},{20,4},{21,5},{22,6},{23,7},{24,8},{25... | collective-permute-start | bytes 1572872 | tf_op jit(solution)/shard_map/ppermute | solution.py:58
  182.6 54.6 %collective-permute-start.28 = (f32[1024,512]{1,0:T(8,128)S(1)}, f32[1024,512]{1,0:T(8,128)S(1)}, u32[]{:S(2)}, u32[]{:S(2)}) collective-permute-start(f32[1024,512]{1,0:T(8,128)S(1)} %fusion), channel_id=1, source_target_pairs={{0,1},{1,0},{2,3},{3,2},{4,5},{5,4},{6,7},{7,6},{8,9},{9,8},{10,11... | collective-permute-start | bytes 6291464 | tf_op jit(solution)/shard_map/ppermute | solution.py:58
  182.7 15.9 %collective-permute-start.23 = (f32[128,512]{1,0:T(8,128)S(1)}, f32[128,512]{1,0:T(8,128)S(1)}, u32[]{:S(2)}, u32[]{:S(2)}) collective-permute-start(f32[128,512]{1,0:T(8,128)S(1)} %pad_maximum_fusion.5), channel_id=1, source_target_pairs={{0,0},{1,1},{2,16},{3,17},{4,32},{5,33},{6,48},{7,49},{8,64},{9,65... | collective-permute-start | bytes 786440 | tf_op jit(solution)/shard_map/ppermute | solution.py:58
  198.7 9.8 %collective-permute-start.24 = (f32[128,512]{1,0:T(8,128)S(1)}, f32[128,512]{1,0:T(8,128)S(1)}, u32[]{:S(2)}, u32[]{:S(2)}) collective-permute-start(f32[128,512]{1,0:T(8,128)S(1)} %collective-permute-done.23), channel_id=1, source_target_pairs={{0,64},{1,65},{2,66},{3,67},{4,68},{5,69},{6,70},{7,71},{8,72},{9,... | collective-permute-start | bytes 786440 | tf_op jit(solution)/shard_map/ppermute | solution.py:58
  208.5 25.6 %collective-permute-start.25 = (f32[256,512]{1,0:T(8,128)S(1)}, f32[256,512]{1,0:T(8,128)S(1)}, u32[]{:S(2)}, u32[]{:S(2)}) collective-permute-start(f32[256,512]{1,0:T(8,128)S(1)} %constant_dynamic-update-slice_fusion.2.refs_0_), channel_id=1, source_target_pairs={{0,48},{1,49},{2,50},{3,51},{4,52},{5,53},{6,54},{7,55},{8,56},{9,... | collective-permute-start | bytes 1572872 | tf_op jit(solution)/shard_map/ppermute | solution.py:58
  208.5 25.5 %collective-permute-start.26 = (f32[256,512]{1,0:T(8,128)S(1)}, f32[256,512]{1,0:T(8,128)S(1)}, u32[]{:S(2)}, u32[]{:S(2)}) collective-permute-start(f32[256,512]{1,0:T(8,128)S(1)} %constant_dynamic-update-slice_fusion.2.refs_0_), channel_id=1, source_target_pairs={{0,32},{1,33},{2,34},{3,35},{4,36},{5,37},{6,38},{7,39},{8,40},{9,... | collective-permute-start | bytes 1572872 | tf_op jit(solution)/shard_map/ppermute | solution.py:58
  208.6 26.0 %collective-permute-start.27 = (f32[256,512]{1,0:T(8,128)S(1)}, f32[256,512]{1,0:T(8,128)S(1)}, u32[]{:S(2)}, u32[]{:S(2)}) collective-permute-start(f32[256,512]{1,0:T(8,128)S(1)} %constant_dynamic-update-slice_fusion.2.refs_0_), channel_id=1, source_target_pairs={{0,16},{1,17},{2,18},{3,19},{4,20},{5,21},{6,22},{7,23},{8,24},{9,... | collective-permute-start | bytes 1572872 | tf_op jit(solution)/shard_map/ppermute | solution.py:58
  238.2 29.1 %collective-permute-start.29 = (f32[1024,256]{1,0:T(8,128)S(1)}, f32[1024,256]{1,0:T(8,128)S(1)}, u32[]{:S(2)}, u32[]{:S(2)}) collective-permute-start(f32[1024,256]{1,0:T(8,128)S(1)} %convolution_add_fusion), channel_id=1, source_target_pairs={{0,0},{1,2},{2,4},{3,1},{4,6},{5,3},{6,8},{7,5},{8,10},{9,7},{10,1... | collective-permute-start | bytes 3145736 | tf_op jit(solution)/shard_map/ppermute | solution.py:58
  239.6 22.9 %collective-permute-start.32 = (f32[512,256]{1,0:T(8,128)S(1)}, f32[512,256]{1,0:T(8,128)S(1)}, u32[]{:S(2)}, u32[]{:S(2)}) collective-permute-start(f32[512,256]{1,0:T(8,128)S(1)} %convolution_add_fusion.2), channel_id=1, source_target_pairs={{0,16},{1,17},{2,18},{3,19},{4,20},{5,21},{6,22},{7,23},{8,24},{9,... | collective-permute-start | bytes 1572872 | tf_op jit(solution)/shard_map/ppermute | solution.py:58
  244.4 22.0 %collective-permute-start.33 = (f32[512,256]{1,0:T(8,128)S(1)}, f32[512,256]{1,0:T(8,128)S(1)}, u32[]{:S(2)}, u32[]{:S(2)}) collective-permute-start(f32[512,256]{1,0:T(8,128)S(1)} %convolution_add_fusion.3), channel_id=1, source_target_pairs={{16,0},{17,1},{18,2},{19,3},{20,4},{21,5},{22,6},{23,7},{24,8},{25... | collective-permute-start | bytes 1572872 | tf_op jit(solution)/shard_map/ppermute | solution.py:58
  266.6 27.3 %collective-permute-start.34 = (f32[1024,256]{1,0:T(8,128)S(1)}, f32[1024,256]{1,0:T(8,128)S(1)}, u32[]{:S(2)}, u32[]{:S(2)}) collective-permute-start(f32[1024,256]{1,0:T(8,128)S(1)} %pad_maximum_fusion.2), channel_id=1, source_target_pairs={{0,0},{1,2},{2,4},{3,1},{4,6},{5,3},{6,8},{7,5},{8,10},{9,7},{10,1... | collective-permute-start | bytes 3145736 | tf_op jit(solution)/shard_map/ppermute | solution.py:58
  267.4 18.6 %collective-permute-start.30 = (f32[512,256]{1,0:T(8,128)S(1)}, f32[512,256]{1,0:T(8,128)S(1)}, u32[]{:S(2)}, u32[]{:S(2)}) collective-permute-start(f32[512,256]{1,0:T(8,128)S(1)} %get-tuple-element.35), channel_id=1, source_target_pairs={{0,16},{1,17},{2,18},{3,19},{4,20},{5,21},{6,22},{7,23},{8,24},{9,... | collective-permute-start | bytes 1572872 | tf_op jit(solution)/shard_map/ppermute | solution.py:58
  273.8 20.0 %collective-permute-start.31 = (f32[512,256]{1,0:T(8,128)S(1)}, f32[512,256]{1,0:T(8,128)S(1)}, u32[]{:S(2)}, u32[]{:S(2)}) collective-permute-start(f32[512,256]{1,0:T(8,128)S(1)} %get-tuple-element.36), channel_id=1, source_target_pairs={{16,0},{17,1},{18,2},{19,3},{20,4},{21,5},{22,6},{23,7},{24,8},{25... | collective-permute-start | bytes 1572872 | tf_op jit(solution)/shard_map/ppermute | solution.py:58
  (5 other events, 61.5 us)
where the time goes:
time: 297 us; the launch traced here: 296 us
  waiting for transfers between devices  204 us (69%)
  starting transfers between devices  62.1 us (21%)
  matrix products  18.4 us (6%)
  other arithmetic  4.49 us (2%)
  Pallas kernels  3.16 us (1%)
  local copies, waits for them, and re-layouts  3.08 us (1%)
    ppermute x35, waiting for transfers between devices, send(): return lax.ppermute(value, ('row', 'col'), pairs)  204 us
    ppermute x35, starting transfers between devices, send(): return lax.ppermute(value, ('row', 'col'), pairs)  62.1 us
    dot_general x12, matrix products, times(): return jnp.dot(tile, turn, precision=HIGH, preferred_element_type=F32)  11.4 us
    dot_general x2, matrix products, mix(): lax.dot_general(turn, tile, dims, precision=HIGH, preferred_element_type=...  6.99 us
  transfers between devices with their start and end apart: 35, of which 22 were waited for; matrix products, arithmetic and copies ran while one was open for 6% of the time, Pallas kernels for 1%

commit v1 on v0

--- a/solution.py
+++ b/solution.py
@@ -96,18 +96,21 @@
 
 
 def cols_body(*refs):
-    pieces, own, other = refs[:4], refs[4:6], refs[6:8]
+    pieces, own, other = refs[:-4], refs[-4:-2], refs[-2:]
     row, core = lax.axis_index("row"), lax.axis_index("col") % 2
     ring, plane = row % 4, row // 4
 
     def fill(first, second):
-        for j, piece in enumerate(pieces):
+        for j in range(4):
             for part in range(4):
                 at = (ring + j) % 4 * 128 + 64 * jnp.where(core == 0, part % 2, 1 - part % 2)
                 rows = pl.ds(pl.multiple_of(at, 64), 64)
-                taken = slice(part * 64, part * 64 + 64)
+                if len(pieces) == 8:
+                    piece, begin = pieces[j + part // 2 * 4], part % 2 * 64
+                else:
+                    piece, begin = pieces[j], part * 64
                 for half, out in enumerate(first if part < 2 else second):
-                    out[rows, :] = piece[taken, half * H : half * H + H]
+                    out[rows, :] = piece[begin : begin + 64, half * H : half * H + H]
 
     @pl.when(plane == core)
     def _():
@@ -131,13 +134,21 @@
 COL_RING = (along_y(1), along_y(-1), along_y(2), OTHER_HI)
 
 
-def gather(own, ring):
+def gather(own, ring, kind, step):
     forward, backward, opposite, other = ring
     to = lambda value, pairs: send(value, pairs)
-    both = jnp.concatenate([own, to(own, other)])
-    before = to(both, forward)
-    behind = to(both, backward)
-    return [both, behind, to(both, opposite), before]
+    across = to(own, other)
+    if kind + step != "b1":
+        both = jnp.concatenate([own, across])
+        before = to(both, forward)
+        behind = to(both, backward)
+        return [both, behind, to(both, opposite), before]
+    before = to(own, forward)
+    behind = to(own, backward)
+    far = to(own, opposite)
+    across_before = to(across, forward)
+    across_behind = to(across, backward)
+    return [own, behind, far, before, across, across_behind, to(far, other), across_before]
 
 
 def shards(gram, rotations):
@@ -151,10 +162,10 @@
         at = int(step) - 1
         piece = jnp.concatenate([keep[at], got[at]])
         turned = send(piece, TRANSPOSE)
-        (half,) = vmem_call(rows_body, gather(piece, ROW_RING), [(2 * N, N)])
+        (half,) = vmem_call(rows_body, gather(piece, ROW_RING, "a", step), [(2 * N, N)])
         other = send(half, OTHER_CORE)
         (whole,) = vmem_call(join_body, (half, other), [(2 * N, 2 * N)])
-        pieces = gather(turned, COL_RING)
+        pieces = gather(turned, COL_RING, "b", step)
         return whole, vmem_call(cols_body, pieces, [(N, H)] * 4)
 
     def advance(tile, rows, cols):

time: 297 us -> 278 us (0.936)
  waiting for transfers between devices: 204 us -> 188 us
    ppermute x35 -> x38, waiting for transfers between devices: 204 us -> 188 us  [send(): return lax.ppermute(value, ('row', 'col'), pairs)]
    ppermute x35 -> x38, starting transfers between devices: 62.1 us -> 59.7 us  [send(): return lax.ppermute(value, ('row', 'col'), pairs)]
  transfers between devices with their start and end apart: 35 -> 38, of which waited for: 22 -> 25; matrix products, arithmetic and copies ran while one was open for 6% -> 6% of each run, Pallas kernels for 1% -> 1%
where the time goes in v1:
time: 278 us; the launch traced here: 277 us
  waiting for transfers between devices  188 us (68%)
  starting transfers between devices  59.7 us (21%)
  matrix products  18.4 us (7%)
  other arithmetic  4.49 us (2%)
  Pallas kernels  3.16 us (1%)
  local copies, waits for them, and re-layouts  3.04 us (1%)
    ppermute x38, waiting for transfers between devices, send(): return lax.ppermute(value, ('row', 'col'), pairs)  188 us
    ppermute x38, starting transfers between devices, send(): return lax.ppermute(value, ('row', 'col'), pairs)  59.7 us
    dot_general x12, matrix products, times(): return jnp.dot(tile, turn, precision=HIGH, preferred_element_type=F32)  11.4 us
    dot_general x2, matrix products, mix(): lax.dot_general(turn, tile, dims, precision=HIGH, preferred_element_type=...  7 us
  transfers between devices with their start and end apart: 38, of which 25 were waited for; matrix products, arithmetic and copies ran while one was open for 6% of the time, Pallas kernels for 1%

profile of v1, /device:TPU:24, one launch (start us, length us, event | category | flops | bytes accessed | tf_op | source)
XLA Modules:
  0.0 276.9 jit_solution(6742010261536405794)
XLA Ops:
  4.8 6.6 %collective-permute-done.6 = f32[128,512]{1,0:T(8,128)S(1)} collective-permute-done((f32[128,512]{1,0:T(8,128)S(1)}, f32[128,512]{1,0:T(8,128)S(1)}, u32[]{:S(2)}, u32[]{:S(2)}) %collective-permute-start.6) | collective-permute-done | bytes 262176 | tf_op jit(solution)/shard_map/ppermute | solution.py:58
  11.4 2.8 %collective-permute-start.7 = (f32[256,512]{1,0:T(8,128)S(1)}, f32[256,512]{1,0:T(8,128)S(1)}, u32[]{:S(2)}, u32[]{:S(2)}) collective-permute-start(f32[256,512]{1,0:T(8,128)S(1)} %pad_maximum_fusion.4.refs_0_), channel_id=1, source_target_pairs={{0,6},{1,7},{2,0},{3,1},{4,2},{5,3},{6,4},{7,5},{8,14},{9,15},{10,... | collective-permute-start | bytes 1572872 | tf_op jit(solution)/shard_map/ppermute | solution.py:58
  15.9 20.4 %collective-permute-done.7.refs_1_ = f32[256,512]{1,0:T(8,128)S(1)} collective-permute-done((f32[256,512]{1,0:T(8,128)S(1)}, f32[256,512]{1,0:T(8,128)S(1)}, u32[]{:S(2)}, u32[]{:S(2)}) %collective-permute-start.7) | collective-permute-done | bytes 524320 | tf_op jit(solution)/shard_map/ppermute | solution.py:58
  36.3 3.7 %collective-permute-done.9.refs_3_ = f32[256,512]{1,0:T(8,128)S(1)} collective-permute-done((f32[256,512]{1,0:T(8,128)S(1)}, f32[256,512]{1,0:T(8,128)S(1)}, u32[]{:S(2)}, u32[]{:S(2)}) %collective-permute-start.9) | collective-permute-done | bytes 524320 | tf_op jit(solution)/shard_map/ppermute | solution.py:58
  44.7 3.6 %fusion.21 = f32[1024,512]{1,0:T(8,128)S(1)} fusion(f32[1024,1024]{1,0:T(8,128)S(1)} %shard_map.31, f32[1024,512]{1,0:T(8,128)S(1)} %copy-done), kind=kOutput, calls=%fused_computation.49 | convolution fusion | flops 3221225472 | bytes 8388608 | tf_op jit(solution)/shard_map/dot_general | solution.py:126
  50.1 9.7 %collective-permute-done.11.refs_0_ = f32[128,512]{1,0:T(8,128)S(1)} collective-permute-done((f32[128,512]{1,0:T(8,128)S(1)}, f32[128,512]{1,0:T(8,128)S(1)}, u32[]{:S(2)}, u32[]{:S(2)}) %collective-permute-start.11) | collective-permute-done | bytes 262176 | tf_op jit(solution)/shard_map/ppermute | solution.py:58
  59.8 4.4 %collective-permute-start.15 = (f32[128,512]{1,0:T(8,128)S(1)}, f32[128,512]{1,0:T(8,128)S(1)}, u32[]{:S(2)}, u32[]{:S(2)}) collective-permute-start(f32[128,512]{1,0:T(8,128)S(1)} %collective-permute-done.11.refs_0_), channel_id=1, source_target_pairs={{0,64},{1,65},{2,66},{3,67},{4,68},{5,69},{6,70},{7,71},{8,72},{9,... | collective-permute-start | bytes 786440 | tf_op jit(solution)/shard_map/ppermute | solution.py:58
  64.8 5.6 %collective-permute-done.15.refs_4_ = f32[128,512]{1,0:T(8,128)S(1)} collective-permute-done((f32[128,512]{1,0:T(8,128)S(1)}, f32[128,512]{1,0:T(8,128)S(1)}, u32[]{:S(2)}, u32[]{:S(2)}) %collective-permute-start.15) | collective-permute-done | bytes 262176 | tf_op jit(solution)/shard_map/ppermute | solution.py:58
  70.3 3.0 %collective-permute-done.13.refs_2_ = f32[128,512]{1,0:T(8,128)S(1)} collective-permute-done((f32[128,512]{1,0:T(8,128)S(1)}, f32[128,512]{1,0:T(8,128)S(1)}, u32[]{:S(2)}, u32[]{:S(2)}) %collective-permute-start.13) | collective-permute-done | bytes 262176 | tf_op jit(solution)/shard_map/ppermute | solution.py:58
  73.4 7.8 %collective-permute-done.12.refs_1_ = f32[128,512]{1,0:T(8,128)S(1)} collective-permute-done((f32[128,512]{1,0:T(8,128)S(1)}, f32[128,512]{1,0:T(8,128)S(1)}, u32[]{:S(2)}, u32[]{:S(2)}) %collective-permute-start.12) | collective-permute-done | bytes 262176 | tf_op jit(solution)/shard_map/ppermute | solution.py:58
  81.2 6.4 %collective-permute-start.16 = (f32[128,512]{1,0:T(8,128)S(1)}, f32[128,512]{1,0:T(8,128)S(1)}, u32[]{:S(2)}, u32[]{:S(2)}) collective-permute-start(f32[128,512]{1,0:T(8,128)S(1)} %collective-permute-done.15.refs_4_), channel_id=1, source_target_pairs={{0,48},{1,49},{2,50},{3,51},{4,52},{5,53},{6,54},{7,55},{8,56},{9,... | collective-permute-start | bytes 786440 | tf_op jit(solution)/shard_map/ppermute | solution.py:58
  88.0 2.4 collective-permute-done.4.refs_3_
  91.6 4.0 %collective-permute-done.17.refs_6_ = f32[128,512]{1,0:T(8,128)S(1)} collective-permute-done((f32[128,512]{1,0:T(8,128)S(1)}, f32[128,512]{1,0:T(8,128)S(1)}, u32[]{:S(2)}, u32[]{:S(2)}) %collective-permute-start.17) | collective-permute-done | bytes 262176 | tf_op jit(solution)/shard_map/ppermute | solution.py:58
  95.6 3.0 %collective-permute-done.18.refs_7_ = f32[128,512]{1,0:T(8,128)S(1)} collective-permute-done((f32[128,512]{1,0:T(8,128)S(1)}, f32[128,512]{1,0:T(8,128)S(1)}, u32[]{:S(2)}, u32[]{:S(2)}) %collective-permute-start.18) | collective-permute-done | bytes 262176 | tf_op jit(solution)/shard_map/ppermute | solution.py:58
  106.4 3.3 %collective-permute-start.23 = (f32[512,256]{1,0:T(8,128)}, f32[512,256]{1,0:T(8,128)}, u32[]{:S(2)}, u32[]{:S(2)}) collective-permute-start(f32[512,256]{1,0:T(8,128)} %convolution_add_fusion.4), channel_id=1, source_target_pairs={{0,16},{1,17},{2,18},{3,19},{4,20},{5,21},{6,22},{7,23},{8,24},{9,... | collective-permute-start | bytes 1572872 | tf_op jit(solution)/shard_map/ppermute | solution.py:58
  111.1 2.6 collective-permute-start.24
  113.7 16.2 %collective-permute-done.23 = f32[512,256]{1,0:T(8,128)} collective-permute-done((f32[512,256]{1,0:T(8,128)}, f32[512,256]{1,0:T(8,128)}, u32[]{:S(2)}, u32[]{:S(2)}) %collective-permute-start.23) | collective-permute-done | bytes 524320 | tf_op jit(solution)/shard_map/ppermute | solution.py:58
  131.0 2.9 %collective-permute-done.24 = f32[512,256]{1,0:T(8,128)} collective-permute-done((f32[512,256]{1,0:T(8,128)}, f32[512,256]{1,0:T(8,128)}, u32[]{:S(2)}, u32[]{:S(2)}) %collective-permute-start.24) | collective-permute-done | bytes 524320 | tf_op jit(solution)/shard_map/ppermute | solution.py:58
  136.0 5.4 %collective-permute-start.21 = (f32[512,256]{1,0:T(8,128)S(1)}, f32[512,256]{1,0:T(8,128)S(1)}, u32[]{:S(2)}, u32[]{:S(2)}) collective-permute-start(f32[512,256]{1,0:T(8,128)S(1)} %get-tuple-element.39), channel_id=1, source_target_pairs={{0,16},{1,17},{2,18},{3,19},{4,20},{5,21},{6,22},{7,23},{8,24},{9,... | collective-permute-start | bytes 1572872 | tf_op jit(solution)/shard_map/ppermute | solution.py:58
  145.1 10.3 %collective-permute-done.21 = f32[512,256]{1,0:T(8,128)S(1)} collective-permute-done((f32[512,256]{1,0:T(8,128)S(1)}, f32[512,256]{1,0:T(8,128)S(1)}, u32[]{:S(2)}, u32[]{:S(2)}) %collective-permute-start.21) | collective-permute-done | bytes 524320 | tf_op jit(solution)/shard_map/ppermute | solution.py:58
  155.5 4.5 %collective-permute-done.22 = f32[512,256]{1,0:T(8,128)S(1)} collective-permute-done((f32[512,256]{1,0:T(8,128)S(1)}, f32[512,256]{1,0:T(8,128)S(1)}, u32[]{:S(2)}, u32[]{:S(2)}) %collective-permute-start.22) | collective-permute-done | bytes 524320 | tf_op jit(solution)/shard_map/ppermute | solution.py:58
  160.1 3.4 %fusion = f32[1024,512]{1,0:T(8,128)S(1)} fusion(f32[1024,1024]{1,0:T(8,128)S(1)} %shard_map.29, f32[1024,256]{1,0:T(8,128)S(1)} %collective-permute-done.25, f32[512,256]{1,0:T(8,128)S(1)} %get-tuple-element.38, f32[512,256]{1,0:T(8,128)S(1)} %get-tuple-element.37), kind=kOutput, calls=%fused_computation | convolution fusion | flops 3222274048 | bytes 8388608 | tf_op jit(solution)/shard_map/dot_general | solution.py:126
  165.6 14.2 %collective-permute-done.26 = f32[128,512]{1,0:T(8,128)S(1)} collective-permute-done((f32[128,512]{1,0:T(8,128)S(1)}, f32[128,512]{1,0:T(8,128)S(1)}, u32[]{:S(2)}, u32[]{:S(2)}) %collective-permute-start.26) | collective-permute-done | bytes 262176 | tf_op jit(solution)/shard_map/ppermute | solution.py:58
  179.9 9.8 %collective-permute-done.27 = f32[128,512]{1,0:T(8,128)S(1)} collective-permute-done((f32[128,512]{1,0:T(8,128)S(1)}, f32[128,512]{1,0:T(8,128)S(1)}, u32[]{:S(2)}, u32[]{:S(2)}) %collective-permute-start.27) | collective-permute-done | bytes 262176 | tf_op jit(solution)/shard_map/ppermute | solution.py:58
  189.8 3.1 %collective-permute-start.30 = (f32[256,512]{1,0:T(8,128)S(1)}, f32[256,512]{1,0:T(8,128)S(1)}, u32[]{:S(2)}, u32[]{:S(2)}) collective-permute-start(f32[256,512]{1,0:T(8,128)S(1)} %constant_dynamic-update-slice_fusion.refs_0_), channel_id=1, source_target_pairs={{0,16},{1,17},{2,18},{3,19},{4,20},{5,21},{6,22},{7,23},{8,24},{9,... | collective-permute-start | bytes 1572872 | tf_op jit(solution)/shard_map/ppermute | solution.py:58
  193.0 22.2 %collective-permute-done.28.refs_1_ = f32[256,512]{1,0:T(8,128)S(1)} collective-permute-done((f32[256,512]{1,0:T(8,128)S(1)}, f32[256,512]{1,0:T(8,128)S(1)}, u32[]{:S(2)}, u32[]{:S(2)}) %collective-permute-start.28) | collective-permute-done | bytes 524320 | tf_op jit(solution)/shard_map/ppermute | solution.py:58
  220.8 4.2 %collective-permute-start.35 = (f32[512,256]{1,0:T(8,128)S(1)}, f32[512,256]{1,0:T(8,128)S(1)}, u32[]{:S(2)}, u32[]{:S(2)}) collective-permute-start(f32[512,256]{1,0:T(8,128)S(1)} %convolution_add_fusion.2), channel_id=1, source_target_pairs={{0,16},{1,17},{2,18},{3,19},{4,20},{5,21},{6,22},{7,23},{8,24},{9,... | collective-permute-start | bytes 1572872 | tf_op jit(solution)/shard_map/ppermute | solution.py:58
  227.6 15.6 %collective-permute-done.35 = f32[512,256]{1,0:T(8,128)S(1)} collective-permute-done((f32[512,256]{1,0:T(8,128)S(1)}, f32[512,256]{1,0:T(8,128)S(1)}, u32[]{:S(2)}, u32[]{:S(2)}) %collective-permute-start.35) | collective-permute-done | bytes 524320 | tf_op jit(solution)/shard_map/ppermute | solution.py:58
  243.2 4.0 %collective-permute-done.36 = f32[512,256]{1,0:T(8,128)S(1)} collective-permute-done((f32[512,256]{1,0:T(8,128)S(1)}, f32[512,256]{1,0:T(8,128)S(1)}, u32[]{:S(2)}, u32[]{:S(2)}) %collective-permute-start.36) | collective-permute-done | bytes 524320 | tf_op jit(solution)/shard_map/ppermute | solution.py:58
  248.2 6.2 %collective-permute-start.33 = (f32[512,256]{1,0:T(8,128)S(1)}, f32[512,256]{1,0:T(8,128)S(1)}, u32[]{:S(2)}, u32[]{:S(2)}) collective-permute-start(f32[512,256]{1,0:T(8,128)S(1)} %get-tuple-element.35), channel_id=1, source_target_pairs={{0,16},{1,17},{2,18},{3,19},{4,20},{5,21},{6,22},{7,23},{8,24},{9,... | collective-permute-start | bytes 1572872 | tf_op jit(solution)/shard_map/ppermute | solution.py:58
  256.3 10.3 %collective-permute-done.33 = f32[512,256]{1,0:T(8,128)S(1)} collective-permute-done((f32[512,256]{1,0:T(8,128)S(1)}, f32[512,256]{1,0:T(8,128)S(1)}, u32[]{:S(2)}, u32[]{:S(2)}) %collective-permute-start.33) | collective-permute-done | bytes 524320 | tf_op jit(solution)/shard_map/ppermute | solution.py:58
  266.7 7.7 %collective-permute-done.34 = f32[512,256]{1,0:T(8,128)S(1)} collective-permute-done((f32[512,256]{1,0:T(8,128)S(1)}, f32[512,256]{1,0:T(8,128)S(1)}, u32[]{:S(2)}, u32[]{:S(2)}) %collective-permute-start.34) | collective-permute-done | bytes 524320 | tf_op jit(solution)/shard_map/ppermute | solution.py:58
  (88 shorter events, 46.9 us)
Async XLA Ops:
  11.4 24.9 %collective-permute-start.7 = (f32[256,512]{1,0:T(8,128)S(1)}, f32[256,512]{1,0:T(8,128)S(1)}, u32[]{:S(2)}, u32[]{:S(2)}) collective-permute-start(f32[256,512]{1,0:T(8,128)S(1)} %pad_maximum_fusion.4.refs_0_), channel_id=1, source_target_pairs={{0,6},{1,7},{2,0},{3,1},{4,2},{5,3},{6,4},{7,5},{8,14},{9,15},{10,... | collective-permute-start | bytes 1572872 | tf_op jit(solution)/shard_map/ppermute | solution.py:58
  14.3 22.1 %collective-permute-start.8 = (f32[256,512]{1,0:T(8,128)S(1)}, f32[256,512]{1,0:T(8,128)S(1)}, u32[]{:S(2)}, u32[]{:S(2)}) collective-permute-start(f32[256,512]{1,0:T(8,128)S(1)} %pad_maximum_fusion.4.refs_0_), channel_id=1, source_target_pairs={{0,4},{1,5},{2,6},{3,7},{4,0},{5,1},{6,2},{7,3},{8,12},{9,13},{10,... | collective-permute-start | bytes 1572872 | tf_op jit(solution)/shard_map/ppermute | solution.py:58
  15.1 24.9 %collective-permute-start.9 = (f32[256,512]{1,0:T(8,128)S(1)}, f32[256,512]{1,0:T(8,128)S(1)}, u32[]{:S(2)}, u32[]{:S(2)}) collective-permute-start(f32[256,512]{1,0:T(8,128)S(1)} %pad_maximum_fusion.4.refs_0_), channel_id=1, source_target_pairs={{0,2},{1,3},{2,4},{3,5},{4,6},{5,7},{6,0},{7,1},{8,10},{9,11},{10,... | collective-permute-start | bytes 1572872 | tf_op jit(solution)/shard_map/ppermute | solution.py:58
  40.3 19.5 %collective-permute-start.11 = (f32[128,512]{1,0:T(8,128)S(1)}, f32[128,512]{1,0:T(8,128)S(1)}, u32[]{:S(2)}, u32[]{:S(2)}) collective-permute-start(f32[128,512]{1,0:T(8,128)S(1)} %pad_maximum_fusion.6), channel_id=1, source_target_pairs={{0,0},{1,1},{2,16},{3,17},{4,32},{5,33},{6,48},{7,49},{8,64},{9,65... | collective-permute-start | bytes 786440 | tf_op jit(solution)/shard_map/ppermute | solution.py:58
  48.3 52.9 %collective-permute-start.19 = (f32[1024,512]{1,0:T(8,128)S(1)}, f32[1024,512]{1,0:T(8,128)S(1)}, u32[]{:S(2)}, u32[]{:S(2)}) collective-permute-start(f32[1024,512]{1,0:T(8,128)S(1)} %fusion.21), channel_id=1, source_target_pairs={{0,1},{1,0},{2,3},{3,2},{4,5},{5,4},{6,7},{7,6},{8,9},{9,8},{10,11... | collective-permute-start | bytes 6291464 | tf_op jit(solution)/shard_map/ppermute | solution.py:58
  48.5 15.7 %collective-permute-start.1 = (f32[128,512]{1,0:T(8,128)S(1)}, f32[128,512]{1,0:T(8,128)S(1)}, u32[]{:S(2)}, u32[]{:S(2)}) collective-permute-start(f32[128,512]{1,0:T(8,128)S(1)} %pad_maximum_fusion.5), channel_id=1, source_target_pairs={{0,8},{1,9},{2,10},{3,11},{4,12},{5,13},{6,14},{7,15},{8,0},{9,1},... | collective-permute-start | bytes 786440 | tf_op jit(solution)/shard_map/ppermute | solution.py:58
  59.8 10.5 %collective-permute-start.15 = (f32[128,512]{1,0:T(8,128)S(1)}, f32[128,512]{1,0:T(8,128)S(1)}, u32[]{:S(2)}, u32[]{:S(2)}) collective-permute-start(f32[128,512]{1,0:T(8,128)S(1)} %collective-permute-done.11.refs_0_), channel_id=1, source_target_pairs={{0,64},{1,65},{2,66},{3,67},{4,68},{5,69},{6,70},{7,71},{8,72},{9,... | collective-permute-start | bytes 786440 | tf_op jit(solution)/shard_map/ppermute | solution.py:58
  64.2 9.2 %collective-permute-start.13 = (f32[128,512]{1,0:T(8,128)S(1)}, f32[128,512]{1,0:T(8,128)S(1)}, u32[]{:S(2)}, u32[]{:S(2)}) collective-permute-start(f32[128,512]{1,0:T(8,128)S(1)} %collective-permute-done.11.refs_0_), channel_id=1, source_target_pairs={{0,32},{1,33},{2,34},{3,35},{4,36},{5,37},{6,38},{7,39},{8,40},{9,... | collective-permute-start | bytes 786440 | tf_op jit(solution)/shard_map/ppermute | solution.py:58
  64.3 17.0 %collective-permute-start.2 = (f32[256,512]{1,0:T(8,128)S(1)}, f32[256,512]{1,0:T(8,128)S(1)}, u32[]{:S(2)}, u32[]{:S(2)}) collective-permute-start(f32[256,512]{1,0:T(8,128)S(1)} %pad_maximum_fusion.3.refs_0_), channel_id=1, source_target_pairs={{0,6},{1,7},{2,0},{3,1},{4,2},{5,3},{6,4},{7,5},{8,14},{9,15},{10,... | collective-permute-start | bytes 1572872 | tf_op jit(solution)/shard_map/ppermute | solution.py:58
  64.8 22.9 %collective-permute-start.3 = (f32[256,512]{1,0:T(8,128)S(1)}, f32[256,512]{1,0:T(8,128)S(1)}, u32[]{:S(2)}, u32[]{:S(2)}) collective-permute-start(f32[256,512]{1,0:T(8,128)S(1)} %pad_maximum_fusion.3.refs_0_), channel_id=1, source_target_pairs={{0,4},{1,5},{2,6},{3,7},{4,0},{5,1},{6,2},{7,3},{8,12},{9,13},{10,... | collective-permute-start | bytes 1572872 | tf_op jit(solution)/shard_map/ppermute | solution.py:58
  70.3 20.0 %collective-permute-start.4 = (f32[256,512]{1,0:T(8,128)S(1)}, f32[256,512]{1,0:T(8,128)S(1)}, u32[]{:S(2)}, u32[]{:S(2)}) collective-permute-start(f32[256,512]{1,0:T(8,128)S(1)} %pad_maximum_fusion.3.refs_0_), channel_id=1, source_target_pairs={{0,2},{1,3},{2,4},{3,5},{4,6},{5,7},{6,0},{7,1},{8,10},{9,11},{10,... | collective-permute-start | bytes 1572872 | tf_op jit(solution)/shard_map/ppermute | solution.py:58
  81.2 9.8 %collective-permute-start.14 = (f32[128,512]{1,0:T(8,128)S(1)}, f32[128,512]{1,0:T(8,128)S(1)}, u32[]{:S(2)}, u32[]{:S(2)}) collective-permute-start(f32[128,512]{1,0:T(8,128)S(1)} %collective-permute-done.11.refs_0_), channel_id=1, source_target_pairs={{0,16},{1,17},{2,18},{3,19},{4,20},{5,21},{6,22},{7,23},{8,24},{9,... | collective-permute-start | bytes 786440 | tf_op jit(solution)/shard_map/ppermute | solution.py:58
  81.2 10.3 %collective-permute-start.16 = (f32[128,512]{1,0:T(8,128)S(1)}, f32[128,512]{1,0:T(8,128)S(1)}, u32[]{:S(2)}, u32[]{:S(2)}) collective-permute-start(f32[128,512]{1,0:T(8,128)S(1)} %collective-permute-done.15.refs_4_), channel_id=1, source_target_pairs={{0,48},{1,49},{2,50},{3,51},{4,52},{5,53},{6,54},{7,55},{8,56},{9,... | collective-permute-start | bytes 786440 | tf_op jit(solution)/shard_map/ppermute | solution.py:58
  91.0 52.3 %collective-permute-start.5 = (f32[1024,512]{1,0:T(8,128)S(1)}, f32[1024,512]{1,0:T(8,128)}, u32[]{:S(2)}, u32[]{:S(2)}) collective-permute-start(f32[1024,512]{1,0:T(8,128)S(1)} %shard_map.28.own), channel_id=1, source_target_pairs={{0,1},{1,0},{2,3},{3,2},{4,5},{5,4},{6,7},{7,6},{8,9},{9,8},{10,11... | collective-permute-start | bytes 6291464 | tf_op jit(solution)/shard_map/ppermute | solution.py:58
  103.1 32.7 %collective-permute-start.20 = (f32[1024,256]{1,0:T(8,128)}, f32[1024,256]{1,0:T(8,128)S(1)}, u32[]{:S(2)}, u32[]{:S(2)}) collective-permute-start(f32[1024,256]{1,0:T(8,128)} %convolution_add_fusion.1), channel_id=1, source_target_pairs={{0,0},{1,2},{2,4},{3,1},{4,6},{5,3},{6,8},{7,5},{8,10},{9,7},{10,1... | collective-permute-start | bytes 3145736 | tf_op jit(solution)/shard_map/ppermute | solution.py:58
  106.4 23.5 %collective-permute-start.23 = (f32[512,256]{1,0:T(8,128)}, f32[512,256]{1,0:T(8,128)}, u32[]{:S(2)}, u32[]{:S(2)}) collective-permute-start(f32[512,256]{1,0:T(8,128)} %convolution_add_fusion.4), channel_id=1, source_target_pairs={{0,16},{1,17},{2,18},{3,19},{4,20},{5,21},{6,22},{7,23},{8,24},{9,... | collective-permute-start | bytes 1572872 | tf_op jit(solution)/shard_map/ppermute | solution.py:58
  111.1 22.8 %collective-permute-start.24 = (f32[512,256]{1,0:T(8,128)}, f32[512,256]{1,0:T(8,128)}, u32[]{:S(2)}, u32[]{:S(2)}) collective-permute-start(f32[512,256]{1,0:T(8,128)} %convolution_add_fusion.5), channel_id=1, source_target_pairs={{16,0},{17,1},{18,2},{19,3},{20,4},{21,5},{22,6},{23,7},{24,8},{25... | collective-permute-start | bytes 1572872 | tf_op jit(solution)/shard_map/ppermute | solution.py:58
  135.1 25.0 %collective-permute-start.25 = (f32[1024,256]{1,0:T(8,128)S(1)}, f32[1024,256]{1,0:T(8,128)S(1)}, u32[]{:S(2)}, u32[]{:S(2)}) collective-permute-start(f32[1024,256]{1,0:T(8,128)S(1)} %pad_maximum_fusion.1), channel_id=1, source_target_pairs={{0,0},{1,2},{2,4},{3,1},{4,6},{5,3},{6,8},{7,5},{8,10},{9,7},{10,1... | collective-permute-start | bytes 3145736 | tf_op jit(solution)/shard_map/ppermute | solution.py:58
  136.0 19.5 %collective-permute-start.21 = (f32[512,256]{1,0:T(8,128)S(1)}, f32[512,256]{1,0:T(8,128)S(1)}, u32[]{:S(2)}, u32[]{:S(2)}) collective-permute-start(f32[512,256]{1,0:T(8,128)S(1)} %get-tuple-element.39), channel_id=1, source_target_pairs={{0,16},{1,17},{2,18},{3,19},{4,20},{5,21},{6,22},{7,23},{8,24},{9,... | collective-permute-start | bytes 1572872 | tf_op jit(solution)/shard_map/ppermute | solution.py:58
  141.3 18.6 %collective-permute-start.22 = (f32[512,256]{1,0:T(8,128)S(1)}, f32[512,256]{1,0:T(8,128)S(1)}, u32[]{:S(2)}, u32[]{:S(2)}) collective-permute-start(f32[512,256]{1,0:T(8,128)S(1)} %get-tuple-element.40), channel_id=1, source_target_pairs={{16,0},{17,1},{18,2},{19,3},{20,4},{21,5},{22,6},{23,7},{24,8},{25... | collective-permute-start | bytes 1572872 | tf_op jit(solution)/shard_map/ppermute | solution.py:58
  163.6 54.8 %collective-permute-start.31 = (f32[1024,512]{1,0:T(8,128)S(1)}, f32[1024,512]{1,0:T(8,128)S(1)}, u32[]{:S(2)}, u32[]{:S(2)}) collective-permute-start(f32[1024,512]{1,0:T(8,128)S(1)} %fusion), channel_id=1, source_target_pairs={{0,1},{1,0},{2,3},{3,2},{4,5},{5,4},{6,7},{7,6},{8,9},{9,8},{10,11... | collective-permute-start | bytes 6291464 | tf_op jit(solution)/shard_map/ppermute | solution.py:58
  163.7 16.2 %collective-permute-start.26 = (f32[128,512]{1,0:T(8,128)S(1)}, f32[128,512]{1,0:T(8,128)S(1)}, u32[]{:S(2)}, u32[]{:S(2)}) collective-permute-start(f32[128,512]{1,0:T(8,128)S(1)} %pad_maximum_fusion.5), channel_id=1, source_target_pairs={{0,0},{1,1},{2,16},{3,17},{4,32},{5,33},{6,48},{7,49},{8,64},{9,65... | collective-permute-start | bytes 786440 | tf_op jit(solution)/shard_map/ppermute | solution.py:58
  179.8 9.8 %collective-permute-start.27 = (f32[128,512]{1,0:T(8,128)S(1)}, f32[128,512]{1,0:T(8,128)S(1)}, u32[]{:S(2)}, u32[]{:S(2)}) collective-permute-start(f32[128,512]{1,0:T(8,128)S(1)} %collective-permute-done.26), channel_id=1, source_target_pairs={{0,64},{1,65},{2,66},{3,67},{4,68},{5,69},{6,70},{7,71},{8,72},{9,... | collective-permute-start | bytes 786440 | tf_op jit(solution)/shard_map/ppermute | solution.py:58
  189.7 25.6 %collective-permute-start.28 = (f32[256,512]{1,0:T(8,128)S(1)}, f32[256,512]{1,0:T(8,128)S(1)}, u32[]{:S(2)}, u32[]{:S(2)}) collective-permute-start(f32[256,512]{1,0:T(8,128)S(1)} %constant_dynamic-update-slice_fusion.refs_0_), channel_id=1, source_target_pairs={{0,48},{1,49},{2,50},{3,51},{4,52},{5,53},{6,54},{7,55},{8,56},{9,... | collective-permute-start | bytes 1572872 | tf_op jit(solution)/shard_map/ppermute | solution.py:58
  189.7 25.5 %collective-permute-start.29 = (f32[256,512]{1,0:T(8,128)S(1)}, f32[256,512]{1,0:T(8,128)S(1)}, u32[]{:S(2)}, u32[]{:S(2)}) collective-permute-start(f32[256,512]{1,0:T(8,128)S(1)} %constant_dynamic-update-slice_fusion.refs_0_), channel_id=1, source_target_pairs={{0,32},{1,33},{2,34},{3,35},{4,36},{5,37},{6,38},{7,39},{8,40},{9,... | collective-permute-start | bytes 1572872 | tf_op jit(solution)/shard_map/ppermute | solution.py:58
  189.8 26.0 %collective-permute-start.30 = (f32[256,512]{1,0:T(8,128)S(1)}, f32[256,512]{1,0:T(8,128)S(1)}, u32[]{:S(2)}, u32[]{:S(2)}) collective-permute-start(f32[256,512]{1,0:T(8,128)S(1)} %constant_dynamic-update-slice_fusion.refs_0_), channel_id=1, source_target_pairs={{0,16},{1,17},{2,18},{3,19},{4,20},{5,21},{6,22},{7,23},{8,24},{9,... | collective-permute-start | bytes 1572872 | tf_op jit(solution)/shard_map/ppermute | solution.py:58
  219.4 28.6 %collective-permute-start.32 = (f32[1024,256]{1,0:T(8,128)S(1)}, f32[1024,256]{1,0:T(8,128)S(1)}, u32[]{:S(2)}, u32[]{:S(2)}) collective-permute-start(f32[1024,256]{1,0:T(8,128)S(1)} %convolution_add_fusion), channel_id=1, source_target_pairs={{0,0},{1,2},{2,4},{3,1},{4,6},{5,3},{6,8},{7,5},{8,10},{9,7},{10,1... | collective-permute-start | bytes 3145736 | tf_op jit(solution)/shard_map/ppermute | solution.py:58
  220.8 22.3 %collective-permute-start.35 = (f32[512,256]{1,0:T(8,128)S(1)}, f32[512,256]{1,0:T(8,128)S(1)}, u32[]{:S(2)}, u32[]{:S(2)}) collective-permute-start(f32[512,256]{1,0:T(8,128)S(1)} %convolution_add_fusion.2), channel_id=1, source_target_pairs={{0,16},{1,17},{2,18},{3,19},{4,20},{5,21},{6,22},{7,23},{8,24},{9,... | collective-permute-start | bytes 1572872 | tf_op jit(solution)/shard_map/ppermute | solution.py:58
  225.6 21.6 %collective-permute-start.36 = (f32[512,256]{1,0:T(8,128)S(1)}, f32[512,256]{1,0:T(8,128)S(1)}, u32[]{:S(2)}, u32[]{:S(2)}) collective-permute-start(f32[512,256]{1,0:T(8,128)S(1)} %convolution_add_fusion.3), channel_id=1, source_target_pairs={{16,0},{17,1},{18,2},{19,3},{20,4},{21,5},{22,6},{23,7},{24,8},{25... | collective-permute-start | bytes 1572872 | tf_op jit(solution)/shard_map/ppermute | solution.py:58
  247.3 27.2 %collective-permute-start.37 = (f32[1024,256]{1,0:T(8,128)S(1)}, f32[1024,256]{1,0:T(8,128)S(1)}, u32[]{:S(2)}, u32[]{:S(2)}) collective-permute-start(f32[1024,256]{1,0:T(8,128)S(1)} %pad_maximum_fusion.2), channel_id=1, source_target_pairs={{0,0},{1,2},{2,4},{3,1},{4,6},{5,3},{6,8},{7,5},{8,10},{9,7},{10,1... | collective-permute-start | bytes 3145736 | tf_op jit(solution)/shard_map/ppermute | solution.py:58
  248.2 18.5 %collective-permute-start.33 = (f32[512,256]{1,0:T(8,128)S(1)}, f32[512,256]{1,0:T(8,128)S(1)}, u32[]{:S(2)}, u32[]{:S(2)}) collective-permute-start(f32[512,256]{1,0:T(8,128)S(1)} %get-tuple-element.35), channel_id=1, source_target_pairs={{0,16},{1,17},{2,18},{3,19},{4,20},{5,21},{6,22},{7,23},{8,24},{9,... | collective-permute-start | bytes 1572872 | tf_op jit(solution)/shard_map/ppermute | solution.py:58
  254.4 20.0 %collective-permute-start.34 = (f32[512,256]{1,0:T(8,128)S(1)}, f32[512,256]{1,0:T(8,128)S(1)}, u32[]{:S(2)}, u32[]{:S(2)}) collective-permute-start(f32[512,256]{1,0:T(8,128)S(1)} %get-tuple-element.36), channel_id=1, source_target_pairs={{16,0},{17,1},{18,2},{19,3},{20,4},{21,5},{22,6},{23,7},{24,8},{25... | collective-permute-start | bytes 1572872 | tf_op jit(solution)/shard_map/ppermute | solution.py:58
  (8 other events, 85.5 us)

commit v2 on v1

--- a/solution.py
+++ b/solution.py
@@ -119,6 +119,12 @@
     @pl.when(plane != core)
     def _():
         fill(other, own)
+
+
+def rows_moved_body(from_above, from_below, up, down, out):
+    row = lax.axis_index("row")
+    out[0:N, :] = jnp.where(row == 0, down[...], from_above[...])
+    out[N:, :] = jnp.where(row == 7, up[...], from_below[...])
 
 
 def mix(turn, tile):
@@ -182,9 +188,8 @@
         row_down = send(down, ROW_DOWN)
         moved_up = send(moved[:N], ROW_UP)
         moved_down = send(moved[N:], ROW_DOWN)
-        row_up = jnp.where(row == 0, down, row_up)
-        row_down = jnp.where(row == 7, up, row_down)
-        right = send(jnp.concatenate([row_up, row_down]), MOVE_COL)
+        (right,) = vmem_call(rows_moved_body, (row_up, row_down, up, down), [(2 * N, H)])
+        right = send(right, MOVE_COL)
         first = jnp.where(row == 0, moved[N:], moved_up)
         second = jnp.where(row == 7, moved[:N], moved_down)
         return jnp.concatenate([jnp.concatenate([first, second]), right], axis=1)

time: 278 us -> 279 us (level)
  starting transfers between devices: 59.7 us -> 68.2 us
  waiting for transfers between devices: 188 us -> 181 us
    ppermute x38, starting transfers between devices: 59.7 us -> 68.2 us  [send(): return lax.ppermute(value, ('row', 'col'), pairs)]
    ppermute x38, waiting for transfers between devices: 188 us -> 181 us  [send(): return lax.ppermute(value, ('row', 'col'), pairs)]
  transfers between devices with their start and end apart: 38 -> 38, of which waited for: 25 -> 23; matrix products, arithmetic and copies ran while one was open for 6% -> 5% of each run, Pallas kernels for 1% -> 1%
where the time goes in v2:
time: 279 us; the launch traced here: 278 us
  waiting for transfers between devices  181 us (65%)
  starting transfers between devices  68.2 us (24%)
  matrix products  17 us (6%)
  local copies, waits for them, and re-layouts  4.9 us (2%)
  Pallas kernels  3.47 us (1%)
  other arithmetic  3.22 us (1%)
    ppermute x38, waiting for transfers between devices, send(): return lax.ppermute(value, ('row', 'col'), pairs)  181 us
    ppermute x38, starting transfers between devices, send(): return lax.ppermute(value, ('row', 'col'), pairs)  68.2 us
    dot_general x12, matrix products, times(): return jnp.dot(tile, turn, precision=HIGH, preferred_element_type=F32)  8.79 us
    dot_general x2, matrix products, mix(): lax.dot_general(turn, tile, dims, precision=HIGH, preferred_element_type=...  8.24 us
  transfers between devices with their start and end apart: 38, of which 23 were waited for; matrix products, arithmetic and copies ran while one was open for 5% of the time, Pallas kernels for 1%

profile of v2, /device:TPU:24, one launch (start us, length us, event | category | flops | bytes accessed | tf_op | source)
XLA Modules:
  0.0 278.1 jit_solution(2612413746347478030)
XLA Ops:
  4.8 6.6 %collective-permute-done.6 = f32[128,512]{1,0:T(8,128)S(1)} collective-permute-done((f32[128,512]{1,0:T(8,128)S(1)}, f32[128,512]{1,0:T(8,128)S(1)}, u32[]{:S(2)}, u32[]{:S(2)}) %collective-permute-start.6) | collective-permute-done | bytes 262176 | tf_op jit(solution)/shard_map/ppermute | solution.py:58
  11.4 2.8 %collective-permute-start.7 = (f32[256,512]{1,0:T(8,128)S(1)}, f32[256,512]{1,0:T(8,128)S(1)}, u32[]{:S(2)}, u32[]{:S(2)}) collective-permute-start(f32[256,512]{1,0:T(8,128)S(1)} %pad_maximum_fusion.2.refs_0_), channel_id=1, source_target_pairs={{0,6},{1,7},{2,0},{3,1},{4,2},{5,3},{6,4},{7,5},{8,14},{9,15},{10,... | collective-permute-start | bytes 1572872 | tf_op jit(solution)/shard_map/ppermute | solution.py:58
  15.9 20.4 %collective-permute-done.7.refs_1_ = f32[256,512]{1,0:T(8,128)S(1)} collective-permute-done((f32[256,512]{1,0:T(8,128)S(1)}, f32[256,512]{1,0:T(8,128)S(1)}, u32[]{:S(2)}, u32[]{:S(2)}) %collective-permute-start.7) | collective-permute-done | bytes 524320 | tf_op jit(solution)/shard_map/ppermute | solution.py:58
  36.3 3.7 %collective-permute-done.9.refs_3_ = f32[256,512]{1,0:T(8,128)S(1)} collective-permute-done((f32[256,512]{1,0:T(8,128)S(1)}, f32[256,512]{1,0:T(8,128)S(1)}, u32[]{:S(2)}, u32[]{:S(2)}) %collective-permute-start.9) | collective-permute-done | bytes 524320 | tf_op jit(solution)/shard_map/ppermute | solution.py:58
  40.3 2.2 collective-permute-start.11
  44.7 3.6 %fusion.21 = f32[1024,512]{1,0:T(8,128)S(1)} fusion(f32[1024,1024]{1,0:T(8,128)S(1)} %shard_map.31, f32[1024,512]{1,0:T(8,128)S(1)} %copy-done), kind=kOutput, calls=%fused_computation.43 | convolution fusion | flops 3221225472 | bytes 8388608 | tf_op jit(solution)/shard_map/dot_general | solution.py:132
  50.1 9.7 %collective-permute-done.11.refs_0_ = f32[128,512]{1,0:T(8,128)S(1)} collective-permute-done((f32[128,512]{1,0:T(8,128)S(1)}, f32[128,512]{1,0:T(8,128)S(1)}, u32[]{:S(2)}, u32[]{:S(2)}) %collective-permute-start.11) | collective-permute-done | bytes 262176 | tf_op jit(solution)/shard_map/ppermute | solution.py:58
  59.8 4.4 %collective-permute-start.15 = (f32[128,512]{1,0:T(8,128)S(1)}, f32[128,512]{1,0:T(8,128)S(1)}, u32[]{:S(2)}, u32[]{:S(2)}) collective-permute-start(f32[128,512]{1,0:T(8,128)S(1)} %collective-permute-done.11.refs_0_), channel_id=1, source_target_pairs={{0,64},{1,65},{2,66},{3,67},{4,68},{5,69},{6,70},{7,71},{8,72},{9,... | collective-permute-start | bytes 786440 | tf_op jit(solution)/shard_map/ppermute | solution.py:58
  64.8 5.6 %collective-permute-done.15.refs_4_ = f32[128,512]{1,0:T(8,128)S(1)} collective-permute-done((f32[128,512]{1,0:T(8,128)S(1)}, f32[128,512]{1,0:T(8,128)S(1)}, u32[]{:S(2)}, u32[]{:S(2)}) %collective-permute-start.15) | collective-permute-done | bytes 262176 | tf_op jit(solution)/shard_map/ppermute | solution.py:58
  70.3 3.0 %collective-permute-done.13.refs_2_ = f32[128,512]{1,0:T(8,128)S(1)} collective-permute-done((f32[128,512]{1,0:T(8,128)S(1)}, f32[128,512]{1,0:T(8,128)S(1)}, u32[]{:S(2)}, u32[]{:S(2)}) %collective-permute-start.13) | collective-permute-done | bytes 262176 | tf_op jit(solution)/shard_map/ppermute | solution.py:58
  73.4 7.8 %collective-permute-done.12.refs_1_ = f32[128,512]{1,0:T(8,128)S(1)} collective-permute-done((f32[128,512]{1,0:T(8,128)S(1)}, f32[128,512]{1,0:T(8,128)S(1)}, u32[]{:S(2)}, u32[]{:S(2)}) %collective-permute-start.12) | collective-permute-done | bytes 262176 | tf_op jit(solution)/shard_map/ppermute | solution.py:58
  81.2 6.4 %collective-permute-start.16 = (f32[128,512]{1,0:T(8,128)S(1)}, f32[128,512]{1,0:T(8,128)S(1)}, u32[]{:S(2)}, u32[]{:S(2)}) collective-permute-start(f32[128,512]{1,0:T(8,128)S(1)} %collective-permute-done.15.refs_4_), channel_id=1, source_target_pairs={{0,48},{1,49},{2,50},{3,51},{4,52},{5,53},{6,54},{7,55},{8,56},{9,... | collective-permute-start | bytes 786440 | tf_op jit(solution)/shard_map/ppermute | solution.py:58
  88.0 2.4 collective-permute-done.4.refs_3_
  91.6 4.0 %collective-permute-done.17.refs_6_ = f32[128,512]{1,0:T(8,128)S(1)} collective-permute-done((f32[128,512]{1,0:T(8,128)S(1)}, f32[128,512]{1,0:T(8,128)S(1)}, u32[]{:S(2)}, u32[]{:S(2)}) %collective-permute-start.17) | collective-permute-done | bytes 262176 | tf_op jit(solution)/shard_map/ppermute | solution.py:58
  95.6 3.0 %collective-permute-done.18.refs_7_ = f32[128,512]{1,0:T(8,128)S(1)} collective-permute-done((f32[128,512]{1,0:T(8,128)S(1)}, f32[128,512]{1,0:T(8,128)S(1)}, u32[]{:S(2)}, u32[]{:S(2)}) %collective-permute-start.18) | collective-permute-done | bytes 262176 | tf_op jit(solution)/shard_map/ppermute | solution.py:58
  103.5 3.4 %collective-permute-start.24 = (f32[512,256]{1,0:T(8,128)S(1)}, f32[512,256]{1,0:T(8,128)S(1)}, u32[]{:S(2)}, u32[]{:S(2)}) collective-permute-start(f32[512,256]{1,0:T(8,128)S(1)} %convolution_add_fusion.4.down), channel_id=1, source_target_pairs={{16,0},{17,1},{18,2},{19,3},{20,4},{21,5},{22,6},{23,7},{24,8},{25... | collective-permute-start | bytes 1572872 | tf_op jit(solution)/shard_map/ppermute | solution.py:58
  107.5 6.1 %collective-permute-start.23 = (f32[512,256]{1,0:T(8,128)S(1)}, f32[512,256]{1,0:T(8,128)S(1)}, u32[]{:S(2)}, u32[]{:S(2)}) collective-permute-start(f32[512,256]{1,0:T(8,128)S(1)} %convolution_add_fusion.5.up), channel_id=1, source_target_pairs={{0,16},{1,17},{2,18},{3,19},{4,20},{5,21},{6,22},{7,23},{8,24},{9,... | collective-permute-start | bytes 1572872 | tf_op jit(solution)/shard_map/ppermute | solution.py:58
  113.6 19.5 %collective-permute-done.24.from_below = f32[512,256]{1,0:T(8,128)S(1)} collective-permute-done((f32[512,256]{1,0:T(8,128)S(1)}, f32[512,256]{1,0:T(8,128)S(1)}, u32[]{:S(2)}, u32[]{:S(2)}) %collective-permute-start.24) | collective-permute-done | bytes 524320 | tf_op jit(solution)/shard_map/ppermute | solution.py:58
  136.9 6.4 %collective-permute-start.21 = (f32[512,256]{1,0:T(8,128)}, f32[512,256]{1,0:T(8,128)}, u32[]{:S(2)}, u32[]{:S(2)}) collective-permute-start(f32[512,256]{1,0:T(8,128)} %get-tuple-element.39), channel_id=1, source_target_pairs={{0,16},{1,17},{2,18},{3,19},{4,20},{5,21},{6,22},{7,23},{8,24},{9,... | collective-permute-start | bytes 1572872 | tf_op jit(solution)/shard_map/ppermute | solution.py:58
  147.2 6.0 %collective-permute-done.21 = f32[512,256]{1,0:T(8,128)} collective-permute-done((f32[512,256]{1,0:T(8,128)}, f32[512,256]{1,0:T(8,128)}, u32[]{:S(2)}, u32[]{:S(2)}) %collective-permute-start.21) | collective-permute-done | bytes 524320 | tf_op jit(solution)/shard_map/ppermute | solution.py:58
  153.3 7.7 %collective-permute-done.22 = f32[512,256]{1,0:T(8,128)} collective-permute-done((f32[512,256]{1,0:T(8,128)}, f32[512,256]{1,0:T(8,128)}, u32[]{:S(2)}, u32[]{:S(2)}) %collective-permute-start.22) | collective-permute-done | bytes 524320 | tf_op jit(solution)/shard_map/ppermute | solution.py:58
  162.4 4.7 %fusion = f32[1024,512]{1,0:T(8,128)S(1)} fusion(f32[1024,1024]{1,0:T(8,128)S(1)} %shard_map.29, f32[1024,256]{1,0:T(8,128)} %collective-permute-done.25, f32[512,256]{1,0:T(8,128)S(1)} %get-tuple-element.38, f32[512,256]{1,0:T(8,128)S(1)} %get-tuple-element.37), kind=kOutput, calls=%fused_computation | convolution fusion | flops 3222274048 | bytes 8388608 | tf_op jit(solution)/shard_map/dot_general | solution.py:132
  169.1 14.0 %collective-permute-done.26 = f32[128,512]{1,0:T(8,128)S(1)} collective-permute-done((f32[128,512]{1,0:T(8,128)S(1)}, f32[128,512]{1,0:T(8,128)S(1)}, u32[]{:S(2)}, u32[]{:S(2)}) %collective-permute-start.26) | collective-permute-done | bytes 262176 | tf_op jit(solution)/shard_map/ppermute | solution.py:58
  183.1 9.8 %collective-permute-done.27 = f32[128,512]{1,0:T(8,128)S(1)} collective-permute-done((f32[128,512]{1,0:T(8,128)S(1)}, f32[128,512]{1,0:T(8,128)S(1)}, u32[]{:S(2)}, u32[]{:S(2)}) %collective-permute-start.27) | collective-permute-done | bytes 262176 | tf_op jit(solution)/shard_map/ppermute | solution.py:58
  193.1 3.1 %collective-permute-start.30 = (f32[256,512]{1,0:T(8,128)S(1)}, f32[256,512]{1,0:T(8,128)S(1)}, u32[]{:S(2)}, u32[]{:S(2)}) collective-permute-start(f32[256,512]{1,0:T(8,128)S(1)} %constant_dynamic-update-slice_fusion.refs_0_), channel_id=1, source_target_pairs={{0,16},{1,17},{2,18},{3,19},{4,20},{5,21},{6,22},{7,23},{8,24},{9,... | collective-permute-start | bytes 1572872 | tf_op jit(solution)/shard_map/ppermute | solution.py:58
  196.2 22.2 %collective-permute-done.28.refs_1_ = f32[256,512]{1,0:T(8,128)S(1)} collective-permute-done((f32[256,512]{1,0:T(8,128)S(1)}, f32[256,512]{1,0:T(8,128)S(1)}, u32[]{:S(2)}, u32[]{:S(2)}) %collective-permute-start.28) | collective-permute-done | bytes 524320 | tf_op jit(solution)/shard_map/ppermute | solution.py:58
  224.0 2.1 collective-permute-start.36
  226.8 7.3 %collective-permute-start.35 = (f32[512,256]{1,0:T(8,128)S(1)}, f32[512,256]{1,0:T(8,128)S(1)}, u32[]{:S(2)}, u32[]{:S(2)}) collective-permute-start(f32[512,256]{1,0:T(8,128)S(1)} %convolution_add_fusion.3.up), channel_id=1, source_target_pairs={{0,16},{1,17},{2,18},{3,19},{4,20},{5,21},{6,22},{7,23},{8,24},{9,... | collective-permute-start | bytes 1572872 | tf_op jit(solution)/shard_map/ppermute | solution.py:58
  234.1 15.7 %collective-permute-done.36.from_below = f32[512,256]{1,0:T(8,128)S(1)} collective-permute-done((f32[512,256]{1,0:T(8,128)S(1)}, f32[512,256]{1,0:T(8,128)S(1)}, u32[]{:S(2)}, u32[]{:S(2)}) %collective-permute-start.36) | collective-permute-done | bytes 524320 | tf_op jit(solution)/shard_map/ppermute | solution.py:58
  250.7 6.9 %collective-permute-start.33 = (f32[512,256]{1,0:T(8,128)S(1)}, f32[512,256]{1,0:T(8,128)S(1)}, u32[]{:S(2)}, u32[]{:S(2)}) collective-permute-start(f32[512,256]{1,0:T(8,128)S(1)} %get-tuple-element.35), channel_id=1, source_target_pairs={{0,16},{1,17},{2,18},{3,19},{4,20},{5,21},{6,22},{7,23},{8,24},{9,... | collective-permute-start | bytes 1572872 | tf_op jit(solution)/shard_map/ppermute | solution.py:58
  259.6 9.3 %collective-permute-done.33 = f32[512,256]{1,0:T(8,128)S(1)} collective-permute-done((f32[512,256]{1,0:T(8,128)S(1)}, f32[512,256]{1,0:T(8,128)S(1)}, u32[]{:S(2)}, u32[]{:S(2)}) %collective-permute-start.33) | collective-permute-done | bytes 524320 | tf_op jit(solution)/shard_map/ppermute | solution.py:58
  268.9 6.8 %collective-permute-done.34 = f32[512,256]{1,0:T(8,128)S(1)} collective-permute-done((f32[512,256]{1,0:T(8,128)S(1)}, f32[512,256]{1,0:T(8,128)S(1)}, u32[]{:S(2)}, u32[]{:S(2)}) %collective-permute-start.34) | collective-permute-done | bytes 524320 | tf_op jit(solution)/shard_map/ppermute | solution.py:58
  (88 shorter events, 40.9 us)
Async XLA Ops:
  11.4 24.9 %collective-permute-start.7 = (f32[256,512]{1,0:T(8,128)S(1)}, f32[256,512]{1,0:T(8,128)S(1)}, u32[]{:S(2)}, u32[]{:S(2)}) collective-permute-start(f32[256,512]{1,0:T(8,128)S(1)} %pad_maximum_fusion.2.refs_0_), channel_id=1, source_target_pairs={{0,6},{1,7},{2,0},{3,1},{4,2},{5,3},{6,4},{7,5},{8,14},{9,15},{10,... | collective-permute-start | bytes 1572872 | tf_op jit(solution)/shard_map/ppermute | solution.py:58
  14.3 22.1 %collective-permute-start.8 = (f32[256,512]{1,0:T(8,128)S(1)}, f32[256,512]{1,0:T(8,128)S(1)}, u32[]{:S(2)}, u32[]{:S(2)}) collective-permute-start(f32[256,512]{1,0:T(8,128)S(1)} %pad_maximum_fusion.2.refs_0_), channel_id=1, source_target_pairs={{0,4},{1,5},{2,6},{3,7},{4,0},{5,1},{6,2},{7,3},{8,12},{9,13},{10,... | collective-permute-start | bytes 1572872 | tf_op jit(solution)/shard_map/ppermute | solution.py:58
  15.1 24.9 %collective-permute-start.9 = (f32[256,512]{1,0:T(8,128)S(1)}, f32[256,512]{1,0:T(8,128)S(1)}, u32[]{:S(2)}, u32[]{:S(2)}) collective-permute-start(f32[256,512]{1,0:T(8,128)S(1)} %pad_maximum_fusion.2.refs_0_), channel_id=1, source_target_pairs={{0,2},{1,3},{2,4},{3,5},{4,6},{5,7},{6,0},{7,1},{8,10},{9,11},{10,... | collective-permute-start | bytes 1572872 | tf_op jit(solution)/shard_map/ppermute | solution.py:58
  40.3 19.5 %collective-permute-start.11 = (f32[128,512]{1,0:T(8,128)S(1)}, f32[128,512]{1,0:T(8,128)S(1)}, u32[]{:S(2)}, u32[]{:S(2)}) collective-permute-start(f32[128,512]{1,0:T(8,128)S(1)} %pad_maximum_fusion.4), channel_id=1, source_target_pairs={{0,0},{1,1},{2,16},{3,17},{4,32},{5,33},{6,48},{7,49},{8,64},{9,65... | collective-permute-start | bytes 786440 | tf_op jit(solution)/shard_map/ppermute | solution.py:58
  48.3 52.9 %collective-permute-start.19 = (f32[1024,512]{1,0:T(8,128)S(1)}, f32[1024,512]{1,0:T(8,128)S(1)}, u32[]{:S(2)}, u32[]{:S(2)}) collective-permute-start(f32[1024,512]{1,0:T(8,128)S(1)} %fusion.21), channel_id=1, source_target_pairs={{0,1},{1,0},{2,3},{3,2},{4,5},{5,4},{6,7},{7,6},{8,9},{9,8},{10,11... | collective-permute-start | bytes 6291464 | tf_op jit(solution)/shard_map/ppermute | solution.py:58
  48.5 15.7 %collective-permute-start.1 = (f32[128,512]{1,0:T(8,128)S(1)}, f32[128,512]{1,0:T(8,128)S(1)}, u32[]{:S(2)}, u32[]{:S(2)}) collective-permute-start(f32[128,512]{1,0:T(8,128)S(1)} %pad_maximum_fusion.3), channel_id=1, source_target_pairs={{0,8},{1,9},{2,10},{3,11},{4,12},{5,13},{6,14},{7,15},{8,0},{9,1},... | collective-permute-start | bytes 786440 | tf_op jit(solution)/shard_map/ppermute | solution.py:58
  59.8 10.5 %collective-permute-start.15 = (f32[128,512]{1,0:T(8,128)S(1)}, f32[128,512]{1,0:T(8,128)S(1)}, u32[]{:S(2)}, u32[]{:S(2)}) collective-permute-start(f32[128,512]{1,0:T(8,128)S(1)} %collective-permute-done.11.refs_0_), channel_id=1, source_target_pairs={{0,64},{1,65},{2,66},{3,67},{4,68},{5,69},{6,70},{7,71},{8,72},{9,... | collective-permute-start | bytes 786440 | tf_op jit(solution)/shard_map/ppermute | solution.py:58
  64.2 9.2 %collective-permute-start.13 = (f32[128,512]{1,0:T(8,128)S(1)}, f32[128,512]{1,0:T(8,128)S(1)}, u32[]{:S(2)}, u32[]{:S(2)}) collective-permute-start(f32[128,512]{1,0:T(8,128)S(1)} %collective-permute-done.11.refs_0_), channel_id=1, source_target_pairs={{0,32},{1,33},{2,34},{3,35},{4,36},{5,37},{6,38},{7,39},{8,40},{9,... | collective-permute-start | bytes 786440 | tf_op jit(solution)/shard_map/ppermute | solution.py:58
  64.3 17.0 %collective-permute-start.2 = (f32[256,512]{1,0:T(8,128)S(1)}, f32[256,512]{1,0:T(8,128)S(1)}, u32[]{:S(2)}, u32[]{:S(2)}) collective-permute-start(f32[256,512]{1,0:T(8,128)S(1)} %pad_maximum_fusion.1.refs_0_), channel_id=1, source_target_pairs={{0,6},{1,7},{2,0},{3,1},{4,2},{5,3},{6,4},{7,5},{8,14},{9,15},{10,... | collective-permute-start | bytes 1572872 | tf_op jit(solution)/shard_map/ppermute | solution.py:58
  64.8 22.9 %collective-permute-start.3 = (f32[256,512]{1,0:T(8,128)S(1)}, f32[256,512]{1,0:T(8,128)S(1)}, u32[]{:S(2)}, u32[]{:S(2)}) collective-permute-start(f32[256,512]{1,0:T(8,128)S(1)} %pad_maximum_fusion.1.refs_0_), channel_id=1, source_target_pairs={{0,4},{1,5},{2,6},{3,7},{4,0},{5,1},{6,2},{7,3},{8,12},{9,13},{10,... | collective-permute-start | bytes 1572872 | tf_op jit(solution)/shard_map/ppermute | solution.py:58
  70.3 20.0 %collective-permute-start.4 = (f32[256,512]{1,0:T(8,128)S(1)}, f32[256,512]{1,0:T(8,128)S(1)}, u32[]{:S(2)}, u32[]{:S(2)}) collective-permute-start(f32[256,512]{1,0:T(8,128)S(1)} %pad_maximum_fusion.1.refs_0_), channel_id=1, source_target_pairs={{0,2},{1,3},{2,4},{3,5},{4,6},{5,7},{6,0},{7,1},{8,10},{9,11},{10,... | collective-permute-start | bytes 1572872 | tf_op jit(solution)/shard_map/ppermute | solution.py:58
  81.2 9.8 %collective-permute-start.14 = (f32[128,512]{1,0:T(8,128)S(1)}, f32[128,512]{1,0:T(8,128)S(1)}, u32[]{:S(2)}, u32[]{:S(2)}) collective-permute-start(f32[128,512]{1,0:T(8,128)S(1)} %collective-permute-done.11.refs_0_), channel_id=1, source_target_pairs={{0,16},{1,17},{2,18},{3,19},{4,20},{5,21},{6,22},{7,23},{8,24},{9,... | collective-permute-start | bytes 786440 | tf_op jit(solution)/shard_map/ppermute | solution.py:58
  81.2 10.3 %collective-permute-start.16 = (f32[128,512]{1,0:T(8,128)S(1)}, f32[128,512]{1,0:T(8,128)S(1)}, u32[]{:S(2)}, u32[]{:S(2)}) collective-permute-start(f32[128,512]{1,0:T(8,128)S(1)} %collective-permute-done.15.refs_4_), channel_id=1, source_target_pairs={{0,48},{1,49},{2,50},{3,51},{4,52},{5,53},{6,54},{7,55},{8,56},{9,... | collective-permute-start | bytes 786440 | tf_op jit(solution)/shard_map/ppermute | solution.py:58
  91.0 54.3 %collective-permute-start.5 = (f32[1024,512]{1,0:T(8,128)S(1)}, f32[1024,512]{1,0:T(8,128)}, u32[]{:S(2)}, u32[]{:S(2)}) collective-permute-start(f32[1024,512]{1,0:T(8,128)S(1)} %shard_map.28.own), channel_id=1, source_target_pairs={{0,1},{1,0},{2,3},{3,2},{4,5},{5,4},{6,7},{7,6},{8,9},{9,8},{10,11... | collective-permute-start | bytes 6291464 | tf_op jit(solution)/shard_map/ppermute | solution.py:58
  102.2 32.7 %collective-permute-start.20 = (f32[1024,256]{1,0:T(8,128)S(1)}, f32[1024,256]{1,0:T(8,128)S(1)}, u32[]{:S(2)}, u32[]{:S(2)}) collective-permute-start(f32[1024,256]{1,0:T(8,128)S(1)} %convolution_add_fusion.1), channel_id=1, source_target_pairs={{0,0},{1,2},{2,4},{3,1},{4,6},{5,3},{6,8},{7,5},{8,10},{9,7},{10,1... | collective-permute-start | bytes 3145736 | tf_op jit(solution)/shard_map/ppermute | solution.py:58
  103.5 29.6 %collective-permute-start.24 = (f32[512,256]{1,0:T(8,128)S(1)}, f32[512,256]{1,0:T(8,128)S(1)}, u32[]{:S(2)}, u32[]{:S(2)}) collective-permute-start(f32[512,256]{1,0:T(8,128)S(1)} %convolution_add_fusion.4.down), channel_id=1, source_target_pairs={{16,0},{17,1},{18,2},{19,3},{20,4},{21,5},{22,6},{23,7},{24,8},{25... | collective-permute-start | bytes 1572872 | tf_op jit(solution)/shard_map/ppermute | solution.py:58
  107.5 25.6 %collective-permute-start.23 = (f32[512,256]{1,0:T(8,128)S(1)}, f32[512,256]{1,0:T(8,128)S(1)}, u32[]{:S(2)}, u32[]{:S(2)}) collective-permute-start(f32[512,256]{1,0:T(8,128)S(1)} %convolution_add_fusion.5.up), channel_id=1, source_target_pairs={{0,16},{1,17},{2,18},{3,19},{4,20},{5,21},{6,22},{7,23},{8,24},{9,... | collective-permute-start | bytes 1572872 | tf_op jit(solution)/shard_map/ppermute | solution.py:58
  133.2 29.1 %collective-permute-start.25 = (f32[1024,256]{1,0:T(8,128)S(1)}, f32[1024,256]{1,0:T(8,128)}, u32[]{:S(2)}, u32[]{:S(2)}) collective-permute-start(f32[1024,256]{1,0:T(8,128)S(1)} %shard_map.33), channel_id=1, source_target_pairs={{0,0},{1,2},{2,4},{3,1},{4,6},{5,3},{6,8},{7,5},{8,10},{9,7},{10,1... | collective-permute-start | bytes 3145736 | tf_op jit(solution)/shard_map/ppermute | solution.py:58
  136.9 16.4 %collective-permute-start.21 = (f32[512,256]{1,0:T(8,128)}, f32[512,256]{1,0:T(8,128)}, u32[]{:S(2)}, u32[]{:S(2)}) collective-permute-start(f32[512,256]{1,0:T(8,128)} %get-tuple-element.39), channel_id=1, source_target_pairs={{0,16},{1,17},{2,18},{3,19},{4,20},{5,21},{6,22},{7,23},{8,24},{9,... | collective-permute-start | bytes 1572872 | tf_op jit(solution)/shard_map/ppermute | solution.py:58
  143.3 17.7 %collective-permute-start.22 = (f32[512,256]{1,0:T(8,128)}, f32[512,256]{1,0:T(8,128)}, u32[]{:S(2)}, u32[]{:S(2)}) collective-permute-start(f32[512,256]{1,0:T(8,128)} %get-tuple-element.40), channel_id=1, source_target_pairs={{16,0},{17,1},{18,2},{19,3},{20,4},{21,5},{22,6},{23,7},{24,8},{25... | collective-permute-start | bytes 1572872 | tf_op jit(solution)/shard_map/ppermute | solution.py:58
  167.1 54.6 %collective-permute-start.31 = (f32[1024,512]{1,0:T(8,128)S(1)}, f32[1024,512]{1,0:T(8,128)S(1)}, u32[]{:S(2)}, u32[]{:S(2)}) collective-permute-start(f32[1024,512]{1,0:T(8,128)S(1)} %fusion), channel_id=1, source_target_pairs={{0,1},{1,0},{2,3},{3,2},{4,5},{5,4},{6,7},{7,6},{8,9},{9,8},{10,11... | collective-permute-start | bytes 6291464 | tf_op jit(solution)/shard_map/ppermute | solution.py:58
  167.1 15.9 %collective-permute-start.26 = (f32[128,512]{1,0:T(8,128)S(1)}, f32[128,512]{1,0:T(8,128)S(1)}, u32[]{:S(2)}, u32[]{:S(2)}) collective-permute-start(f32[128,512]{1,0:T(8,128)S(1)} %pad_maximum_fusion.3), channel_id=1, source_target_pairs={{0,0},{1,1},{2,16},{3,17},{4,32},{5,33},{6,48},{7,49},{8,64},{9,65... | collective-permute-start | bytes 786440 | tf_op jit(solution)/shard_map/ppermute | solution.py:58
  183.1 9.8 %collective-permute-start.27 = (f32[128,512]{1,0:T(8,128)S(1)}, f32[128,512]{1,0:T(8,128)S(1)}, u32[]{:S(2)}, u32[]{:S(2)}) collective-permute-start(f32[128,512]{1,0:T(8,128)S(1)} %collective-permute-done.26), channel_id=1, source_target_pairs={{0,64},{1,65},{2,66},{3,67},{4,68},{5,69},{6,70},{7,71},{8,72},{9,... | collective-permute-start | bytes 786440 | tf_op jit(solution)/shard_map/ppermute | solution.py:58
  192.9 25.6 %collective-permute-start.28 = (f32[256,512]{1,0:T(8,128)S(1)}, f32[256,512]{1,0:T(8,128)S(1)}, u32[]{:S(2)}, u32[]{:S(2)}) collective-permute-start(f32[256,512]{1,0:T(8,128)S(1)} %constant_dynamic-update-slice_fusion.refs_0_), channel_id=1, source_target_pairs={{0,48},{1,49},{2,50},{3,51},{4,52},{5,53},{6,54},{7,55},{8,56},{9,... | collective-permute-start | bytes 1572872 | tf_op jit(solution)/shard_map/ppermute | solution.py:58
  193.0 25.5 %collective-permute-start.29 = (f32[256,512]{1,0:T(8,128)S(1)}, f32[256,512]{1,0:T(8,128)S(1)}, u32[]{:S(2)}, u32[]{:S(2)}) collective-permute-start(f32[256,512]{1,0:T(8,128)S(1)} %constant_dynamic-update-slice_fusion.refs_0_), channel_id=1, source_target_pairs={{0,32},{1,33},{2,34},{3,35},{4,36},{5,37},{6,38},{7,39},{8,40},{9,... | collective-permute-start | bytes 1572872 | tf_op jit(solution)/shard_map/ppermute | solution.py:58
  193.1 26.0 %collective-permute-start.30 = (f32[256,512]{1,0:T(8,128)S(1)}, f32[256,512]{1,0:T(8,128)S(1)}, u32[]{:S(2)}, u32[]{:S(2)}) collective-permute-start(f32[256,512]{1,0:T(8,128)S(1)} %constant_dynamic-update-slice_fusion.refs_0_), channel_id=1, source_target_pairs={{0,16},{1,17},{2,18},{3,19},{4,20},{5,21},{6,22},{7,23},{8,24},{9,... | collective-permute-start | bytes 1572872 | tf_op jit(solution)/shard_map/ppermute | solution.py:58
  222.7 28.0 %collective-permute-start.32 = (f32[1024,256]{1,0:T(8,128)S(1)}, f32[1024,256]{1,0:T(8,128)S(1)}, u32[]{:S(2)}, u32[]{:S(2)}) collective-permute-start(f32[1024,256]{1,0:T(8,128)S(1)} %convolution_add_fusion), channel_id=1, source_target_pairs={{0,0},{1,2},{2,4},{3,1},{4,6},{5,3},{6,8},{7,5},{8,10},{9,7},{10,1... | collective-permute-start | bytes 3145736 | tf_op jit(solution)/shard_map/ppermute | solution.py:58
  224.0 25.8 %collective-permute-start.36 = (f32[512,256]{1,0:T(8,128)S(1)}, f32[512,256]{1,0:T(8,128)S(1)}, u32[]{:S(2)}, u32[]{:S(2)}) collective-permute-start(f32[512,256]{1,0:T(8,128)S(1)} %convolution_add_fusion.2.down), channel_id=1, source_target_pairs={{16,0},{17,1},{18,2},{19,3},{20,4},{21,5},{22,6},{23,7},{24,8},{25... | collective-permute-start | bytes 1572872 | tf_op jit(solution)/shard_map/ppermute | solution.py:58
  226.8 23.0 %collective-permute-start.35 = (f32[512,256]{1,0:T(8,128)S(1)}, f32[512,256]{1,0:T(8,128)S(1)}, u32[]{:S(2)}, u32[]{:S(2)}) collective-permute-start(f32[512,256]{1,0:T(8,128)S(1)} %convolution_add_fusion.3.up), channel_id=1, source_target_pairs={{0,16},{1,17},{2,18},{3,19},{4,20},{5,21},{6,22},{7,23},{8,24},{9,... | collective-permute-start | bytes 1572872 | tf_op jit(solution)/shard_map/ppermute | solution.py:58
  249.9 25.9 %collective-permute-start.37 = (f32[1024,256]{1,0:T(8,128)S(1)}, f32[1024,256]{1,0:T(8,128)S(1)}, u32[]{:S(2)}, u32[]{:S(2)}) collective-permute-start(f32[1024,256]{1,0:T(8,128)S(1)} %shard_map.35), channel_id=1, source_target_pairs={{0,0},{1,2},{2,4},{3,1},{4,6},{5,3},{6,8},{7,5},{8,10},{9,7},{10,1... | collective-permute-start | bytes 3145736 | tf_op jit(solution)/shard_map/ppermute | solution.py:58
  250.7 18.2 %collective-permute-start.33 = (f32[512,256]{1,0:T(8,128)S(1)}, f32[512,256]{1,0:T(8,128)S(1)}, u32[]{:S(2)}, u32[]{:S(2)}) collective-permute-start(f32[512,256]{1,0:T(8,128)S(1)} %get-tuple-element.35), channel_id=1, source_target_pairs={{0,16},{1,17},{2,18},{3,19},{4,20},{5,21},{6,22},{7,23},{8,24},{9,... | collective-permute-start | bytes 1572872 | tf_op jit(solution)/shard_map/ppermute | solution.py:58
  257.7 18.0 %collective-permute-start.34 = (f32[512,256]{1,0:T(8,128)S(1)}, f32[512,256]{1,0:T(8,128)S(1)}, u32[]{:S(2)}, u32[]{:S(2)}) collective-permute-start(f32[512,256]{1,0:T(8,128)S(1)} %get-tuple-element.36), channel_id=1, source_target_pairs={{16,0},{17,1},{18,2},{19,3},{20,4},{21,5},{22,6},{23,7},{24,8},{25... | collective-permute-start | bytes 1572872 | tf_op jit(solution)/shard_map/ppermute | solution.py:58
  (10 other events, 102.1 us)

commit v3 on v2

--- a/solution.py
+++ b/solution.py
@@ -174,7 +174,7 @@
         pieces = gather(turned, COL_RING, "b", step)
         return whole, vmem_call(cols_body, pieces, [(N, H)] * 4)
 
-    def advance(tile, rows, cols):
+    def advance(step, tile, rows, cols):
         own_a, own_b, other_a, other_b = cols
         mixed = mix(rows, tile)
         other = send(mixed, OTHER_CORE)
@@ -188,7 +188,11 @@
         row_down = send(down, ROW_DOWN)
         moved_up = send(moved[:N], ROW_UP)
         moved_down = send(moved[N:], ROW_DOWN)
-        (right,) = vmem_call(rows_moved_body, (row_up, row_down, up, down), [(2 * N, H)])
+        if step == "2":
+            (right,) = vmem_call(rows_moved_body, (row_up, row_down, up, down), [(2 * N, H)])
+        else:
+            row_up = jnp.where(row == 0, down, row_up)
+            right = jnp.concatenate([row_up, jnp.where(row == 7, up, row_down)])
         right = send(right, MOVE_COL)
         first = jnp.where(row == 0, moved[N:], moved_up)
         second = jnp.where(row == 7, moved[:N], moved_down)
@@ -196,7 +200,7 @@
 
     tile = gram
     for step in ("1", "2"):
-        tile = advance(tile, *turns(step))
+        tile = advance(step, tile, *turns(step))
     return tile
 
 

time: 279 us -> 276 us (0.989)
  starting transfers between devices: 68.2 us -> 63.1 us
    ppermute x38, starting transfers between devices: 68.2 us -> 63.1 us  [send(): return lax.ppermute(value, ('row', 'col'), pairs)]
  transfers between devices with their start and end apart: 38 -> 38, of which waited for: 23 -> 24; matrix products, arithmetic and copies ran while one was open for 5% -> 6% of each run, Pallas kernels for 1% -> 1%
where the time goes in v3:
time: 276 us; the launch traced here: 274 us
  waiting for transfers between devices  181 us (66%)
  starting transfers between devices  63.1 us (23%)
  matrix products  18.4 us (7%)
  other arithmetic  4.31 us (2%)
  Pallas kernels  3.27 us (1%)
  local copies, waits for them, and re-layouts  2.96 us (1%)
    ppermute x38, waiting for transfers between devices, send(): return lax.ppermute(value, ('row', 'col'), pairs)  181 us
    ppermute x38, starting transfers between devices, send(): return lax.ppermute(value, ('row', 'col'), pairs)  63.1 us
    dot_general x12, matrix products, times(): return jnp.dot(tile, turn, precision=HIGH, preferred_element_type=F32)  11.4 us
    dot_general x2, matrix products, mix(): lax.dot_general(turn, tile, dims, precision=HIGH, preferred_element_type=...  7 us
  transfers between devices with their start and end apart: 38, of which 24 were waited for; matrix products, arithmetic and copies ran while one was open for 6% of the time, Pallas kernels for 1%

profile of v3, /device:TPU:24, one launch (start us, length us, event | category | flops | bytes accessed | tf_op | source)
XLA Modules:
  0.0 273.8 jit_solution(17581404939762472972)
XLA Ops:
  4.8 6.6 %collective-permute-done.6 = f32[128,512]{1,0:T(8,128)S(1)} collective-permute-done((f32[128,512]{1,0:T(8,128)S(1)}, f32[128,512]{1,0:T(8,128)S(1)}, u32[]{:S(2)}, u32[]{:S(2)}) %collective-permute-start.6) | collective-permute-done | bytes 262176 | tf_op jit(solution)/shard_map/ppermute | solution.py:58
  11.4 2.8 %collective-permute-start.7 = (f32[256,512]{1,0:T(8,128)S(1)}, f32[256,512]{1,0:T(8,128)S(1)}, u32[]{:S(2)}, u32[]{:S(2)}) collective-permute-start(f32[256,512]{1,0:T(8,128)S(1)} %pad_maximum_fusion.3.refs_0_), channel_id=1, source_target_pairs={{0,6},{1,7},{2,0},{3,1},{4,2},{5,3},{6,4},{7,5},{8,14},{9,15},{10,... | collective-permute-start | bytes 1572872 | tf_op jit(solution)/shard_map/ppermute | solution.py:58
  15.9 20.4 %collective-permute-done.7.refs_1_ = f32[256,512]{1,0:T(8,128)S(1)} collective-permute-done((f32[256,512]{1,0:T(8,128)S(1)}, f32[256,512]{1,0:T(8,128)S(1)}, u32[]{:S(2)}, u32[]{:S(2)}) %collective-permute-start.7) | collective-permute-done | bytes 524320 | tf_op jit(solution)/shard_map/ppermute | solution.py:58
  36.3 3.7 %collective-permute-done.9.refs_3_ = f32[256,512]{1,0:T(8,128)S(1)} collective-permute-done((f32[256,512]{1,0:T(8,128)S(1)}, f32[256,512]{1,0:T(8,128)S(1)}, u32[]{:S(2)}, u32[]{:S(2)}) %collective-permute-start.9) | collective-permute-done | bytes 524320 | tf_op jit(solution)/shard_map/ppermute | solution.py:58
  40.3 2.2 collective-permute-start.11
  44.7 3.6 %fusion.21 = f32[1024,512]{1,0:T(8,128)S(1)} fusion(f32[1024,1024]{1,0:T(8,128)S(1)} %shard_map.31, f32[1024,512]{1,0:T(8,128)S(1)} %copy-done), kind=kOutput, calls=%fused_computation.46 | convolution fusion | flops 3221225472 | bytes 8388608 | tf_op jit(solution)/shard_map/dot_general | solution.py:132
  50.1 9.7 %collective-permute-done.11.refs_0_ = f32[128,512]{1,0:T(8,128)S(1)} collective-permute-done((f32[128,512]{1,0:T(8,128)S(1)}, f32[128,512]{1,0:T(8,128)S(1)}, u32[]{:S(2)}, u32[]{:S(2)}) %collective-permute-start.11) | collective-permute-done | bytes 262176 | tf_op jit(solution)/shard_map/ppermute | solution.py:58
  59.8 4.4 %collective-permute-start.15 = (f32[128,512]{1,0:T(8,128)S(1)}, f32[128,512]{1,0:T(8,128)S(1)}, u32[]{:S(2)}, u32[]{:S(2)}) collective-permute-start(f32[128,512]{1,0:T(8,128)S(1)} %collective-permute-done.11.refs_0_), channel_id=1, source_target_pairs={{0,64},{1,65},{2,66},{3,67},{4,68},{5,69},{6,70},{7,71},{8,72},{9,... | collective-permute-start | bytes 786440 | tf_op jit(solution)/shard_map/ppermute | solution.py:58
  64.8 5.6 %collective-permute-done.15.refs_4_ = f32[128,512]{1,0:T(8,128)S(1)} collective-permute-done((f32[128,512]{1,0:T(8,128)S(1)}, f32[128,512]{1,0:T(8,128)S(1)}, u32[]{:S(2)}, u32[]{:S(2)}) %collective-permute-start.15) | collective-permute-done | bytes 262176 | tf_op jit(solution)/shard_map/ppermute | solution.py:58
  70.3 3.0 %collective-permute-done.13.refs_2_ = f32[128,512]{1,0:T(8,128)S(1)} collective-permute-done((f32[128,512]{1,0:T(8,128)S(1)}, f32[128,512]{1,0:T(8,128)S(1)}, u32[]{:S(2)}, u32[]{:S(2)}) %collective-permute-start.13) | collective-permute-done | bytes 262176 | tf_op jit(solution)/shard_map/ppermute | solution.py:58
  73.4 7.8 %collective-permute-done.12.refs_1_ = f32[128,512]{1,0:T(8,128)S(1)} collective-permute-done((f32[128,512]{1,0:T(8,128)S(1)}, f32[128,512]{1,0:T(8,128)S(1)}, u32[]{:S(2)}, u32[]{:S(2)}) %collective-permute-start.12) | collective-permute-done | bytes 262176 | tf_op jit(solution)/shard_map/ppermute | solution.py:58
  81.2 6.4 %collective-permute-start.16 = (f32[128,512]{1,0:T(8,128)S(1)}, f32[128,512]{1,0:T(8,128)S(1)}, u32[]{:S(2)}, u32[]{:S(2)}) collective-permute-start(f32[128,512]{1,0:T(8,128)S(1)} %collective-permute-done.15.refs_4_), channel_id=1, source_target_pairs={{0,48},{1,49},{2,50},{3,51},{4,52},{5,53},{6,54},{7,55},{8,56},{9,... | collective-permute-start | bytes 786440 | tf_op jit(solution)/shard_map/ppermute | solution.py:58
  88.0 2.4 collective-permute-done.4.refs_3_
  91.6 4.0 %collective-permute-done.17.refs_6_ = f32[128,512]{1,0:T(8,128)S(1)} collective-permute-done((f32[128,512]{1,0:T(8,128)S(1)}, f32[128,512]{1,0:T(8,128)S(1)}, u32[]{:S(2)}, u32[]{:S(2)}) %collective-permute-start.17) | collective-permute-done | bytes 262176 | tf_op jit(solution)/shard_map/ppermute | solution.py:58
  95.6 3.0 %collective-permute-done.18.refs_7_ = f32[128,512]{1,0:T(8,128)S(1)} collective-permute-done((f32[128,512]{1,0:T(8,128)S(1)}, f32[128,512]{1,0:T(8,128)S(1)}, u32[]{:S(2)}, u32[]{:S(2)}) %collective-permute-start.18) | collective-permute-done | bytes 262176 | tf_op jit(solution)/shard_map/ppermute | solution.py:58
  106.4 3.3 %collective-permute-start.23 = (f32[512,256]{1,0:T(8,128)}, f32[512,256]{1,0:T(8,128)}, u32[]{:S(2)}, u32[]{:S(2)}) collective-permute-start(f32[512,256]{1,0:T(8,128)} %convolution_add_fusion.4), channel_id=1, source_target_pairs={{0,16},{1,17},{2,18},{3,19},{4,20},{5,21},{6,22},{7,23},{8,24},{9,... | collective-permute-start | bytes 1572872 | tf_op jit(solution)/shard_map/ppermute | solution.py:58
  111.1 2.6 collective-permute-start.24
  113.7 16.2 %collective-permute-done.23 = f32[512,256]{1,0:T(8,128)} collective-permute-done((f32[512,256]{1,0:T(8,128)}, f32[512,256]{1,0:T(8,128)}, u32[]{:S(2)}, u32[]{:S(2)}) %collective-permute-start.23) | collective-permute-done | bytes 524320 | tf_op jit(solution)/shard_map/ppermute | solution.py:58
  131.0 2.9 %collective-permute-done.24 = f32[512,256]{1,0:T(8,128)} collective-permute-done((f32[512,256]{1,0:T(8,128)}, f32[512,256]{1,0:T(8,128)}, u32[]{:S(2)}, u32[]{:S(2)}) %collective-permute-start.24) | collective-permute-done | bytes 524320 | tf_op jit(solution)/shard_map/ppermute | solution.py:58
  136.0 5.4 %collective-permute-start.21 = (f32[512,256]{1,0:T(8,128)S(1)}, f32[512,256]{1,0:T(8,128)S(1)}, u32[]{:S(2)}, u32[]{:S(2)}) collective-permute-start(f32[512,256]{1,0:T(8,128)S(1)} %get-tuple-element.39), channel_id=1, source_target_pairs={{0,16},{1,17},{2,18},{3,19},{4,20},{5,21},{6,22},{7,23},{8,24},{9,... | collective-permute-start | bytes 1572872 | tf_op jit(solution)/shard_map/ppermute | solution.py:58
  145.1 10.3 %collective-permute-done.21 = f32[512,256]{1,0:T(8,128)S(1)} collective-permute-done((f32[512,256]{1,0:T(8,128)S(1)}, f32[512,256]{1,0:T(8,128)S(1)}, u32[]{:S(2)}, u32[]{:S(2)}) %collective-permute-start.21) | collective-permute-done | bytes 524320 | tf_op jit(solution)/shard_map/ppermute | solution.py:58
  155.5 4.5 %collective-permute-done.22 = f32[512,256]{1,0:T(8,128)S(1)} collective-permute-done((f32[512,256]{1,0:T(8,128)S(1)}, f32[512,256]{1,0:T(8,128)S(1)}, u32[]{:S(2)}, u32[]{:S(2)}) %collective-permute-start.22) | collective-permute-done | bytes 524320 | tf_op jit(solution)/shard_map/ppermute | solution.py:58
  160.1 3.4 %fusion = f32[1024,512]{1,0:T(8,128)S(1)} fusion(f32[1024,1024]{1,0:T(8,128)S(1)} %shard_map.29, f32[1024,256]{1,0:T(8,128)S(1)} %collective-permute-done.25, f32[512,256]{1,0:T(8,128)S(1)} %get-tuple-element.38, f32[512,256]{1,0:T(8,128)S(1)} %get-tuple-element.37), kind=kOutput, calls=%fused_computation | convolution fusion | flops 3222274048 | bytes 8388608 | tf_op jit(solution)/shard_map/dot_general | solution.py:132
  165.6 14.2 %collective-permute-done.26 = f32[128,512]{1,0:T(8,128)S(1)} collective-permute-done((f32[128,512]{1,0:T(8,128)S(1)}, f32[128,512]{1,0:T(8,128)S(1)}, u32[]{:S(2)}, u32[]{:S(2)}) %collective-permute-start.26) | collective-permute-done | bytes 262176 | tf_op jit(solution)/shard_map/ppermute | solution.py:58
  179.9 9.8 %collective-permute-done.27 = f32[128,512]{1,0:T(8,128)S(1)} collective-permute-done((f32[128,512]{1,0:T(8,128)S(1)}, f32[128,512]{1,0:T(8,128)S(1)}, u32[]{:S(2)}, u32[]{:S(2)}) %collective-permute-start.27) | collective-permute-done | bytes 262176 | tf_op jit(solution)/shard_map/ppermute | solution.py:58
  189.8 3.1 %collective-permute-start.30 = (f32[256,512]{1,0:T(8,128)S(1)}, f32[256,512]{1,0:T(8,128)S(1)}, u32[]{:S(2)}, u32[]{:S(2)}) collective-permute-start(f32[256,512]{1,0:T(8,128)S(1)} %constant_dynamic-update-slice_fusion.refs_0_), channel_id=1, source_target_pairs={{0,16},{1,17},{2,18},{3,19},{4,20},{5,21},{6,22},{7,23},{8,24},{9,... | collective-permute-start | bytes 1572872 | tf_op jit(solution)/shard_map/ppermute | solution.py:58
  193.0 22.2 %collective-permute-done.28.refs_1_ = f32[256,512]{1,0:T(8,128)S(1)} collective-permute-done((f32[256,512]{1,0:T(8,128)S(1)}, f32[256,512]{1,0:T(8,128)S(1)}, u32[]{:S(2)}, u32[]{:S(2)}) %collective-permute-start.28) | collective-permute-done | bytes 524320 | tf_op jit(solution)/shard_map/ppermute | solution.py:58
  223.6 7.3 %collective-permute-start.35 = (f32[512,256]{1,0:T(8,128)S(1)}, f32[512,256]{1,0:T(8,128)S(1)}, u32[]{:S(2)}, u32[]{:S(2)}) collective-permute-start(f32[512,256]{1,0:T(8,128)S(1)} %convolution_add_fusion.3.up), channel_id=1, source_target_pairs={{0,16},{1,17},{2,18},{3,19},{4,20},{5,21},{6,22},{7,23},{8,24},{9,... | collective-permute-start | bytes 1572872 | tf_op jit(solution)/shard_map/ppermute | solution.py:58
  230.9 16.3 %collective-permute-done.36.from_below = f32[512,256]{1,0:T(8,128)S(1)} collective-permute-done((f32[512,256]{1,0:T(8,128)S(1)}, f32[512,256]{1,0:T(8,128)S(1)}, u32[]{:S(2)}, u32[]{:S(2)}) %collective-permute-start.36) | collective-permute-done | bytes 524320 | tf_op jit(solution)/shard_map/ppermute | solution.py:58
  248.1 6.4 %collective-permute-start.33 = (f32[512,256]{1,0:T(8,128)S(1)}, f32[512,256]{1,0:T(8,128)S(1)}, u32[]{:S(2)}, u32[]{:S(2)}) collective-permute-start(f32[512,256]{1,0:T(8,128)S(1)} %get-tuple-element.35), channel_id=1, source_target_pairs={{0,16},{1,17},{2,18},{3,19},{4,20},{5,21},{6,22},{7,23},{8,24},{9,... | collective-permute-start | bytes 1572872 | tf_op jit(solution)/shard_map/ppermute | solution.py:58
  256.4 8.7 %collective-permute-done.33 = f32[512,256]{1,0:T(8,128)S(1)} collective-permute-done((f32[512,256]{1,0:T(8,128)S(1)}, f32[512,256]{1,0:T(8,128)S(1)}, u32[]{:S(2)}, u32[]{:S(2)}) %collective-permute-start.33) | collective-permute-done | bytes 524320 | tf_op jit(solution)/shard_map/ppermute | solution.py:58
  265.1 6.2 %collective-permute-done.34 = f32[512,256]{1,0:T(8,128)S(1)} collective-permute-done((f32[512,256]{1,0:T(8,128)S(1)}, f32[512,256]{1,0:T(8,128)S(1)}, u32[]{:S(2)}, u32[]{:S(2)}) %collective-permute-start.34) | collective-permute-done | bytes 524320 | tf_op jit(solution)/shard_map/ppermute | solution.py:58
  (86 shorter events, 44.8 us)
Async XLA Ops:
  11.4 24.9 %collective-permute-start.7 = (f32[256,512]{1,0:T(8,128)S(1)}, f32[256,512]{1,0:T(8,128)S(1)}, u32[]{:S(2)}, u32[]{:S(2)}) collective-permute-start(f32[256,512]{1,0:T(8,128)S(1)} %pad_maximum_fusion.3.refs_0_), channel_id=1, source_target_pairs={{0,6},{1,7},{2,0},{3,1},{4,2},{5,3},{6,4},{7,5},{8,14},{9,15},{10,... | collective-permute-start | bytes 1572872 | tf_op jit(solution)/shard_map/ppermute | solution.py:58
  14.3 22.1 %collective-permute-start.8 = (f32[256,512]{1,0:T(8,128)S(1)}, f32[256,512]{1,0:T(8,128)S(1)}, u32[]{:S(2)}, u32[]{:S(2)}) collective-permute-start(f32[256,512]{1,0:T(8,128)S(1)} %pad_maximum_fusion.3.refs_0_), channel_id=1, source_target_pairs={{0,4},{1,5},{2,6},{3,7},{4,0},{5,1},{6,2},{7,3},{8,12},{9,13},{10,... | collective-permute-start | bytes 1572872 | tf_op jit(solution)/shard_map/ppermute | solution.py:58
  15.1 24.9 %collective-permute-start.9 = (f32[256,512]{1,0:T(8,128)S(1)}, f32[256,512]{1,0:T(8,128)S(1)}, u32[]{:S(2)}, u32[]{:S(2)}) collective-permute-start(f32[256,512]{1,0:T(8,128)S(1)} %pad_maximum_fusion.3.refs_0_), channel_id=1, source_target_pairs={{0,2},{1,3},{2,4},{3,5},{4,6},{5,7},{6,0},{7,1},{8,10},{9,11},{10,... | collective-permute-start | bytes 1572872 | tf_op jit(solution)/shard_map/ppermute | solution.py:58
  40.3 19.5 %collective-permute-start.11 = (f32[128,512]{1,0:T(8,128)S(1)}, f32[128,512]{1,0:T(8,128)S(1)}, u32[]{:S(2)}, u32[]{:S(2)}) collective-permute-start(f32[128,512]{1,0:T(8,128)S(1)} %pad_maximum_fusion.5), channel_id=1, source_target_pairs={{0,0},{1,1},{2,16},{3,17},{4,32},{5,33},{6,48},{7,49},{8,64},{9,65... | collective-permute-start | bytes 786440 | tf_op jit(solution)/shard_map/ppermute | solution.py:58
  48.3 52.9 %collective-permute-start.19 = (f32[1024,512]{1,0:T(8,128)S(1)}, f32[1024,512]{1,0:T(8,128)S(1)}, u32[]{:S(2)}, u32[]{:S(2)}) collective-permute-start(f32[1024,512]{1,0:T(8,128)S(1)} %fusion.21), channel_id=1, source_target_pairs={{0,1},{1,0},{2,3},{3,2},{4,5},{5,4},{6,7},{7,6},{8,9},{9,8},{10,11... | collective-permute-start | bytes 6291464 | tf_op jit(solution)/shard_map/ppermute | solution.py:58
  48.5 15.7 %collective-permute-start.1 = (f32[128,512]{1,0:T(8,128)S(1)}, f32[128,512]{1,0:T(8,128)S(1)}, u32[]{:S(2)}, u32[]{:S(2)}) collective-permute-start(f32[128,512]{1,0:T(8,128)S(1)} %pad_maximum_fusion.4), channel_id=1, source_target_pairs={{0,8},{1,9},{2,10},{3,11},{4,12},{5,13},{6,14},{7,15},{8,0},{9,1},... | collective-permute-start | bytes 786440 | tf_op jit(solution)/shard_map/ppermute | solution.py:58
  59.8 10.5 %collective-permute-start.15 = (f32[128,512]{1,0:T(8,128)S(1)}, f32[128,512]{1,0:T(8,128)S(1)}, u32[]{:S(2)}, u32[]{:S(2)}) collective-permute-start(f32[128,512]{1,0:T(8,128)S(1)} %collective-permute-done.11.refs_0_), channel_id=1, source_target_pairs={{0,64},{1,65},{2,66},{3,67},{4,68},{5,69},{6,70},{7,71},{8,72},{9,... | collective-permute-start | bytes 786440 | tf_op jit(solution)/shard_map/ppermute | solution.py:58
  64.2 9.2 %collective-permute-start.13 = (f32[128,512]{1,0:T(8,128)S(1)}, f32[128,512]{1,0:T(8,128)S(1)}, u32[]{:S(2)}, u32[]{:S(2)}) collective-permute-start(f32[128,512]{1,0:T(8,128)S(1)} %collective-permute-done.11.refs_0_), channel_id=1, source_target_pairs={{0,32},{1,33},{2,34},{3,35},{4,36},{5,37},{6,38},{7,39},{8,40},{9,... | collective-permute-start | bytes 786440 | tf_op jit(solution)/shard_map/ppermute | solution.py:58
  64.3 17.0 %collective-permute-start.2 = (f32[256,512]{1,0:T(8,128)S(1)}, f32[256,512]{1,0:T(8,128)S(1)}, u32[]{:S(2)}, u32[]{:S(2)}) collective-permute-start(f32[256,512]{1,0:T(8,128)S(1)} %pad_maximum_fusion.2.refs_0_), channel_id=1, source_target_pairs={{0,6},{1,7},{2,0},{3,1},{4,2},{5,3},{6,4},{7,5},{8,14},{9,15},{10,... | collective-permute-start | bytes 1572872 | tf_op jit(solution)/shard_map/ppermute | solution.py:58
  64.8 22.9 %collective-permute-start.3 = (f32[256,512]{1,0:T(8,128)S(1)}, f32[256,512]{1,0:T(8,128)S(1)}, u32[]{:S(2)}, u32[]{:S(2)}) collective-permute-start(f32[256,512]{1,0:T(8,128)S(1)} %pad_maximum_fusion.2.refs_0_), channel_id=1, source_target_pairs={{0,4},{1,5},{2,6},{3,7},{4,0},{5,1},{6,2},{7,3},{8,12},{9,13},{10,... | collective-permute-start | bytes 1572872 | tf_op jit(solution)/shard_map/ppermute | solution.py:58
  70.3 20.0 %collective-permute-start.4 = (f32[256,512]{1,0:T(8,128)S(1)}, f32[256,512]{1,0:T(8,128)S(1)}, u32[]{:S(2)}, u32[]{:S(2)}) collective-permute-start(f32[256,512]{1,0:T(8,128)S(1)} %pad_maximum_fusion.2.refs_0_), channel_id=1, source_target_pairs={{0,2},{1,3},{2,4},{3,5},{4,6},{5,7},{6,0},{7,1},{8,10},{9,11},{10,... | collective-permute-start | bytes 1572872 | tf_op jit(solution)/shard_map/ppermute | solution.py:58
  81.2 9.8 %collective-permute-start.14 = (f32[128,512]{1,0:T(8,128)S(1)}, f32[128,512]{1,0:T(8,128)S(1)}, u32[]{:S(2)}, u32[]{:S(2)}) collective-permute-start(f32[128,512]{1,0:T(8,128)S(1)} %collective-permute-done.11.refs_0_), channel_id=1, source_target_pairs={{0,16},{1,17},{2,18},{3,19},{4,20},{5,21},{6,22},{7,23},{8,24},{9,... | collective-permute-start | bytes 786440 | tf_op jit(solution)/shard_map/ppermute | solution.py:58
  81.2 10.3 %collective-permute-start.16 = (f32[128,512]{1,0:T(8,128)S(1)}, f32[128,512]{1,0:T(8,128)S(1)}, u32[]{:S(2)}, u32[]{:S(2)}) collective-permute-start(f32[128,512]{1,0:T(8,128)S(1)} %collective-permute-done.15.refs_4_), channel_id=1, source_target_pairs={{0,48},{1,49},{2,50},{3,51},{4,52},{5,53},{6,54},{7,55},{8,56},{9,... | collective-permute-start | bytes 786440 | tf_op jit(solution)/shard_map/ppermute | solution.py:58
  91.0 52.3 %collective-permute-start.5 = (f32[1024,512]{1,0:T(8,128)S(1)}, f32[1024,512]{1,0:T(8,128)}, u32[]{:S(2)}, u32[]{:S(2)}) collective-permute-start(f32[1024,512]{1,0:T(8,128)S(1)} %shard_map.28.own), channel_id=1, source_target_pairs={{0,1},{1,0},{2,3},{3,2},{4,5},{5,4},{6,7},{7,6},{8,9},{9,8},{10,11... | collective-permute-start | bytes 6291464 | tf_op jit(solution)/shard_map/ppermute | solution.py:58
  103.1 32.7 %collective-permute-start.20 = (f32[1024,256]{1,0:T(8,128)}, f32[1024,256]{1,0:T(8,128)S(1)}, u32[]{:S(2)}, u32[]{:S(2)}) collective-permute-start(f32[1024,256]{1,0:T(8,128)} %convolution_add_fusion.1), channel_id=1, source_target_pairs={{0,0},{1,2},{2,4},{3,1},{4,6},{5,3},{6,8},{7,5},{8,10},{9,7},{10,1... | collective-permute-start | bytes 3145736 | tf_op jit(solution)/shard_map/ppermute | solution.py:58
  106.4 23.5 %collective-permute-start.23 = (f32[512,256]{1,0:T(8,128)}, f32[512,256]{1,0:T(8,128)}, u32[]{:S(2)}, u32[]{:S(2)}) collective-permute-start(f32[512,256]{1,0:T(8,128)} %convolution_add_fusion.4), channel_id=1, source_target_pairs={{0,16},{1,17},{2,18},{3,19},{4,20},{5,21},{6,22},{7,23},{8,24},{9,... | collective-permute-start | bytes 1572872 | tf_op jit(solution)/shard_map/ppermute | solution.py:58
  111.1 22.8 %collective-permute-start.24 = (f32[512,256]{1,0:T(8,128)}, f32[512,256]{1,0:T(8,128)}, u32[]{:S(2)}, u32[]{:S(2)}) collective-permute-start(f32[512,256]{1,0:T(8,128)} %convolution_add_fusion.5), channel_id=1, source_target_pairs={{16,0},{17,1},{18,2},{19,3},{20,4},{21,5},{22,6},{23,7},{24,8},{25... | collective-permute-start | bytes 1572872 | tf_op jit(solution)/shard_map/ppermute | solution.py:58
  135.1 25.0 %collective-permute-start.25 = (f32[1024,256]{1,0:T(8,128)S(1)}, f32[1024,256]{1,0:T(8,128)S(1)}, u32[]{:S(2)}, u32[]{:S(2)}) collective-permute-start(f32[1024,256]{1,0:T(8,128)S(1)} %pad_maximum_fusion.1), channel_id=1, source_target_pairs={{0,0},{1,2},{2,4},{3,1},{4,6},{5,3},{6,8},{7,5},{8,10},{9,7},{10,1... | collective-permute-start | bytes 3145736 | tf_op jit(solution)/shard_map/ppermute | solution.py:58
  136.0 19.5 %collective-permute-start.21 = (f32[512,256]{1,0:T(8,128)S(1)}, f32[512,256]{1,0:T(8,128)S(1)}, u32[]{:S(2)}, u32[]{:S(2)}) collective-permute-start(f32[512,256]{1,0:T(8,128)S(1)} %get-tuple-element.39), channel_id=1, source_target_pairs={{0,16},{1,17},{2,18},{3,19},{4,20},{5,21},{6,22},{7,23},{8,24},{9,... | collective-permute-start | bytes 1572872 | tf_op jit(solution)/shard_map/ppermute | solution.py:58
  141.3 18.6 %collective-permute-start.22 = (f32[512,256]{1,0:T(8,128)S(1)}, f32[512,256]{1,0:T(8,128)S(1)}, u32[]{:S(2)}, u32[]{:S(2)}) collective-permute-start(f32[512,256]{1,0:T(8,128)S(1)} %get-tuple-element.40), channel_id=1, source_target_pairs={{16,0},{17,1},{18,2},{19,3},{20,4},{21,5},{22,6},{23,7},{24,8},{25... | collective-permute-start | bytes 1572872 | tf_op jit(solution)/shard_map/ppermute | solution.py:58
  163.6 54.8 %collective-permute-start.31 = (f32[1024,512]{1,0:T(8,128)S(1)}, f32[1024,512]{1,0:T(8,128)S(1)}, u32[]{:S(2)}, u32[]{:S(2)}) collective-permute-start(f32[1024,512]{1,0:T(8,128)S(1)} %fusion), channel_id=1, source_target_pairs={{0,1},{1,0},{2,3},{3,2},{4,5},{5,4},{6,7},{7,6},{8,9},{9,8},{10,11... | collective-permute-start | bytes 6291464 | tf_op jit(solution)/shard_map/ppermute | solution.py:58
  163.7 16.2 %collective-permute-start.26 = (f32[128,512]{1,0:T(8,128)S(1)}, f32[128,512]{1,0:T(8,128)S(1)}, u32[]{:S(2)}, u32[]{:S(2)}) collective-permute-start(f32[128,512]{1,0:T(8,128)S(1)} %pad_maximum_fusion.4), channel_id=1, source_target_pairs={{0,0},{1,1},{2,16},{3,17},{4,32},{5,33},{6,48},{7,49},{8,64},{9,65... | collective-permute-start | bytes 786440 | tf_op jit(solution)/shard_map/ppermute | solution.py:58
  179.8 9.8 %collective-permute-start.27 = (f32[128,512]{1,0:T(8,128)S(1)}, f32[128,512]{1,0:T(8,128)S(1)}, u32[]{:S(2)}, u32[]{:S(2)}) collective-permute-start(f32[128,512]{1,0:T(8,128)S(1)} %collective-permute-done.26), channel_id=1, source_target_pairs={{0,64},{1,65},{2,66},{3,67},{4,68},{5,69},{6,70},{7,71},{8,72},{9,... | collective-permute-start | bytes 786440 | tf_op jit(solution)/shard_map/ppermute | solution.py:58
  189.7 25.6 %collective-permute-start.28 = (f32[256,512]{1,0:T(8,128)S(1)}, f32[256,512]{1,0:T(8,128)S(1)}, u32[]{:S(2)}, u32[]{:S(2)}) collective-permute-start(f32[256,512]{1,0:T(8,128)S(1)} %constant_dynamic-update-slice_fusion.refs_0_), channel_id=1, source_target_pairs={{0,48},{1,49},{2,50},{3,51},{4,52},{5,53},{6,54},{7,55},{8,56},{9,... | collective-permute-start | bytes 1572872 | tf_op jit(solution)/shard_map/ppermute | solution.py:58
  189.7 25.5 %collective-permute-start.29 = (f32[256,512]{1,0:T(8,128)S(1)}, f32[256,512]{1,0:T(8,128)S(1)}, u32[]{:S(2)}, u32[]{:S(2)}) collective-permute-start(f32[256,512]{1,0:T(8,128)S(1)} %constant_dynamic-update-slice_fusion.refs_0_), channel_id=1, source_target_pairs={{0,32},{1,33},{2,34},{3,35},{4,36},{5,37},{6,38},{7,39},{8,40},{9,... | collective-permute-start | bytes 1572872 | tf_op jit(solution)/shard_map/ppermute | solution.py:58
  189.8 26.0 %collective-permute-start.30 = (f32[256,512]{1,0:T(8,128)S(1)}, f32[256,512]{1,0:T(8,128)S(1)}, u32[]{:S(2)}, u32[]{:S(2)}) collective-permute-start(f32[256,512]{1,0:T(8,128)S(1)} %constant_dynamic-update-slice_fusion.refs_0_), channel_id=1, source_target_pairs={{0,16},{1,17},{2,18},{3,19},{4,20},{5,21},{6,22},{7,23},{8,24},{9,... | collective-permute-start | bytes 1572872 | tf_op jit(solution)/shard_map/ppermute | solution.py:58
  219.5 28.6 %collective-permute-start.32 = (f32[1024,256]{1,0:T(8,128)S(1)}, f32[1024,256]{1,0:T(8,128)S(1)}, u32[]{:S(2)}, u32[]{:S(2)}) collective-permute-start(f32[1024,256]{1,0:T(8,128)S(1)} %convolution_add_fusion), channel_id=1, source_target_pairs={{0,0},{1,2},{2,4},{3,1},{4,6},{5,3},{6,8},{7,5},{8,10},{9,7},{10,1... | collective-permute-start | bytes 3145736 | tf_op jit(solution)/shard_map/ppermute | solution.py:58
  220.8 26.4 %collective-permute-start.36 = (f32[512,256]{1,0:T(8,128)S(1)}, f32[512,256]{1,0:T(8,128)S(1)}, u32[]{:S(2)}, u32[]{:S(2)}) collective-permute-start(f32[512,256]{1,0:T(8,128)S(1)} %convolution_add_fusion.2.down), channel_id=1, source_target_pairs={{16,0},{17,1},{18,2},{19,3},{20,4},{21,5},{22,6},{23,7},{24,8},{25... | collective-permute-start | bytes 1572872 | tf_op jit(solution)/shard_map/ppermute | solution.py:58
  223.6 23.6 %collective-permute-start.35 = (f32[512,256]{1,0:T(8,128)S(1)}, f32[512,256]{1,0:T(8,128)S(1)}, u32[]{:S(2)}, u32[]{:S(2)}) collective-permute-start(f32[512,256]{1,0:T(8,128)S(1)} %convolution_add_fusion.3.up), channel_id=1, source_target_pairs={{0,16},{1,17},{2,18},{3,19},{4,20},{5,21},{6,22},{7,23},{8,24},{9,... | collective-permute-start | bytes 1572872 | tf_op jit(solution)/shard_map/ppermute | solution.py:58
  247.3 24.1 %collective-permute-start.37 = (f32[1024,256]{1,0:T(8,128)S(1)}, f32[1024,256]{1,0:T(8,128)S(1)}, u32[]{:S(2)}, u32[]{:S(2)}) collective-permute-start(f32[1024,256]{1,0:T(8,128)S(1)} %shard_map.34), channel_id=1, source_target_pairs={{0,0},{1,2},{2,4},{3,1},{4,6},{5,3},{6,8},{7,5},{8,10},{9,7},{10,1... | collective-permute-start | bytes 3145736 | tf_op jit(solution)/shard_map/ppermute | solution.py:58
  248.1 17.0 %collective-permute-start.33 = (f32[512,256]{1,0:T(8,128)S(1)}, f32[512,256]{1,0:T(8,128)S(1)}, u32[]{:S(2)}, u32[]{:S(2)}) collective-permute-start(f32[512,256]{1,0:T(8,128)S(1)} %get-tuple-element.35), channel_id=1, source_target_pairs={{0,16},{1,17},{2,18},{3,19},{4,20},{5,21},{6,22},{7,23},{8,24},{9,... | collective-permute-start | bytes 1572872 | tf_op jit(solution)/shard_map/ppermute | solution.py:58
  254.5 16.8 %collective-permute-start.34 = (f32[512,256]{1,0:T(8,128)S(1)}, f32[512,256]{1,0:T(8,128)S(1)}, u32[]{:S(2)}, u32[]{:S(2)}) collective-permute-start(f32[512,256]{1,0:T(8,128)S(1)} %get-tuple-element.36), channel_id=1, source_target_pairs={{16,0},{17,1},{18,2},{19,3},{20,4},{21,5},{22,6},{23,7},{24,8},{25... | collective-permute-start | bytes 1572872 | tf_op jit(solution)/shard_map/ppermute | solution.py:58
  (8 other events, 85.4 us)
